TPU v7x, 32 devices: a whole 2x2x4 slice. The times are simulated.
32 devices in a mesh: grp: 2 (over y), slab: 4 (over z), orb: 2 (over x), rep: 2 (over core).
Axes of the slice: x: 2, y: 2, z: 4, core: 2. Of those that a mesh axis runs over, the one named last changes fastest.
Arguments:
- orbitals: bfloat16 [16, 32, 1024], P(('grp', 'slab', 'orb')), parts along dimension 0, may hold values from -6 to 6
- corners: int32 [16, 3], P('grp'), parts along dimension 0, may hold values from 0 to 191, as said below
- partners: int32 [16, 24], P(('grp', 'slab', 'orb')), parts along dimension 0, may hold values from -1 to 7, as said below
- kernel: float32 [32, 1024], replicated, may hold values from 0.05 to 5
Outputs:
- exchange_boxes: float32 [16, 32, 1024], P(('grp', 'slab', 'orb')), parts along dimension 0
- exchange_energy: float32 [2], P('grp'), parts along dimension 0
There are 2 independent parts, one for each index of `grp`. A program takes and returns all parts, laid end to end along the dimension named above; an argument that names none is the same for every part. Nothing has to cross between parts.
Inputs may be any that keep to these rules, and one draw needn't show every extreme that they name: corners[i, 2] lies in the slab of orbital i: from 12 * (i // (1 * 2)) to 12 more less one; corners[i, 0] and corners[i, 1] lie below 192. `partners`: row i starts with i itself, names distinct orbitals whose boxes intersect box i (every component of o is above -32 and below 32), and has its -1 entries only after all others.
All inputs are finite; a program needn't handle non-finite values.
Results may differ from a plain program's by a relative error of at most 0.0003.
Values may be sent and summed in bfloat16 or wider, within the bound.
No kernel may reach another device: no remote copies, remote signals or barrier semaphores. Data moves between devices by JAX's collectives and lax.ppermute only.
A program may use at most 64 MiB of HBM per device.

v0:
```python
import functools
import math

import jax
import jax.numpy as jnp
import numpy as np
from jax import lax
from jax.experimental import pallas as pl
from jax.experimental.pallas import tpu as pltpu
from jax.sharding import PartitionSpec as P

G = 192
ZDEV = 12
PB = 4
RADIX = 4


def passed_along(array, axis, by):
    size = lax.axis_size(axis)
    return lax.ppermute(array, axis, [(i, (i + by) % size) for i in range(size)])


def swapped_sum(value, axes):
    size = math.prod(lax.axis_size(axis) for axis in axes)
    if size & (size - 1) or size > 4:
        return lax.psum(value, axes)
    terms = [value] + [
        lax.ppermute(value, axes, [(i, i ^ d) for i in range(size)]) for d in range(1, size)
    ]
    while len(terms) > 1:
        terms = [terms[i] + terms[i + 1] for i in range(0, len(terms), 2)]
    return terms[0]


def turned_boxes(orbitals):
    axes = ("slab", "orb", "rep")
    slabs, side = lax.axis_size("slab"), lax.axis_size("orb")
    boxes = []
    for d in range(slabs):
        moves = [
            ((s * side + x) * side + r, ((s + d) % slabs * side + r) * side + x)
            for s in range(slabs)
            for x in range(side)
            for r in range(side)
        ]
        boxes.append(lax.ppermute(orbitals, axes, moves))
    return boxes


def halves(table):
    table = np.asarray(table, np.float32)
    high = table.astype(jnp.bfloat16)
    low = (table - high.astype(np.float32)).astype(jnp.bfloat16)
    return np.stack([high, low])


def fourier_tables(box_edge):
    inner = box_edge // RADIX
    unit = 2.0 * np.pi / box_edge
    s, c, q1, r = np.meshgrid(
        np.arange(inner), np.arange(box_edge), np.arange(inner), np.arange(box_edge), indexing="ij"
    )
    tile = inner * box_edge
    plane = []
    for q0 in range(RADIX - 1):
        angle = (((q0 + RADIX * q1) * s + r * c) % box_edge).reshape(tile, tile) * unit
        plane.append(np.concatenate([np.cos(angle), -np.sin(angle)], axis=1))
    ids = np.arange(box_edge)
    edge_angle = (ids[:, None] * ids[None, :] % box_edge) * unit
    cosine = np.kron(np.eye(PB), np.cos(edge_angle))
    sine = np.kron(np.eye(PB), np.sin(edge_angle))
    ahead = np.block([[cosine, sine], [-sine, cosine]])
    return halves(np.stack(plane)), halves(np.stack([ahead, ahead.T]))


def split(values):
    high = values.astype(jnp.bfloat16)
    return high, (values - high.astype(jnp.float32)).astype(jnp.bfloat16)


def product(left, right, dims):
    one = functools.partial(
        lax.dot_general, dimension_numbers=(dims, ((), ())), preferred_element_type=jnp.float32
    )
    return one(left[0], right[0]) + (one(left[1], right[0]) + one(left[0], right[1]))


NN = ((1,), (0,))
NT = ((1,), (1,))


def pair_kernel(*refs, slab_count, orb_count, rep_count, halo_depth, turned):
    partners, corners, own, filters, plane_tab, edge_tab = refs[:6]
    pools = refs[6:-4]
    out, energy, moved_box, chosen = refs[-4:]
    own_count, box_edge, plane = own.shape
    slot_count = partners.shape[1]
    tile = plane // RADIX
    rows = PB * box_edge
    slab_position = lax.axis_index("slab")
    first_own = (slab_position * orb_count + lax.axis_index("orb")) * own_count
    group_size = own_count * orb_count
    lengths = (G, G, ZDEV * slab_count)
    a_ids = lax.broadcasted_iota(jnp.int32, (box_edge, 1), 0)
    lane_ids = lax.broadcasted_iota(jnp.int32, (1, plane), 1)
    b_ids = lane_ids // box_edge
    c_ids = lane_ids % box_edge
    total = jnp.zeros((1, 1), jnp.float32)
    for o in range(own_count):
        centre = own[o].astype(jnp.float32)
        filled = jnp.int32(0)
        for k in range(slot_count):
            partner = partners[o, k]
            column = lax.rem(jnp.maximum(partner, 0) // own_count, orb_count)
            mine = (partner >= 0) & (lax.rem(column, rep_count) == lax.axis_index("rep"))
            chosen[filled] = partner
            filled = filled + mine.astype(jnp.int32)
        out[o] = jnp.zeros((box_edge, plane), jnp.float32)

        def block(step, carry):
            for p in range(PB):
                slot = step * PB + p
                usable = slot < filled
                partner = jnp.where(usable, chosen[jnp.minimum(slot, slot_count - 1)], 0)
                shift = []
                for d in range(3):
                    half = lengths[d] // 2
                    delta = corners[first_own + o, d] - corners[partner, d] + half
                    delta = jnp.where(delta < 0, delta + lengths[d], delta)
                    delta = jnp.where(delta >= lengths[d], delta - lengths[d], delta)
                    shift.append(delta - half)
                slab = partner // group_size
                if turned:
                    away = lax.rem(slab_position - slab + slab_count, slab_count)
                    inner = lax.rem(partner, own_count)
                    box = pools[0][inner]
                    for d in range(1, slab_count):
                        box = jnp.where(away == d, pools[d][inner], box)
                else:
                    away = lax.rem(slab - slab_position + halo_depth + slab_count, slab_count)
                    box = pools[0][away * group_size + lax.rem(partner, group_size)]
                box = box.astype(jnp.float32)
                flat = shift[1] * box_edge + shift[2]
                flat = lax.rem(RADIX * plane - flat, plane)
                box = pltpu.roll(box, flat, 1)
                box = pltpu.roll(box, lax.rem(RADIX * box_edge - shift[0], box_edge), 0)
                a_src = a_ids + shift[0]
                b_src = b_ids + shift[1]
                c_src = c_ids + shift[2]
                in_a = (a_src >= 0) & (a_src < box_edge) & usable
                in_bc = (b_src >= 0) & (b_src < box_edge) & (c_src >= 0) & (c_src < box_edge)
                weight = in_a.astype(jnp.float32) * in_bc.astype(jnp.float32)
                moved_box[p] = box * weight
            density = (moved_box[...] * centre[None]).reshape(rows, plane)
            x0, x1, x2, x3 = (density[:, t * tile:(t + 1) * tile] for t in range(RADIX))
            even, odd = x0 + x2, x1 + x3
            tables = [(plane_tab[0, q], plane_tab[1, q]) for q in range(RADIX - 1)]
            y0 = product(split(even + odd), tables[0], NN)
            y2 = product(split(even - odd), tables[2], NN)
            uv = product(split(jnp.concatenate([x0 - x2, x1 - x3], axis=0)), tables[1], NN)
            y1_re = uv[:rows, :tile] + uv[rows:, tile:]
            y1_im = uv[:rows, tile:] - uv[rows:, :tile]
            spectrum = jnp.concatenate(
                [
                    jnp.concatenate([y0[:, :tile], y1_re, y2[:, :tile]], axis=1),
                    jnp.concatenate([y0[:, tile:], y1_im, y2[:, tile:]], axis=1),
                ],
                axis=0,
            )
            spectrum = product((edge_tab[0, 0], edge_tab[1, 0]), split(spectrum), NN)
            width = spectrum.shape[1]
            spectrum = spectrum.reshape(2 * PB, box_edge, width) * filters[...][None]
            spectrum = spectrum.reshape(2 * rows, width)
            spectrum = product((edge_tab[0, 1], edge_tab[1, 1]), split(spectrum), NN)
            re, im = spectrum[:rows], spectrum[rows:]
            pick = lambda part, q: part[:, q * tile:(q + 1) * tile]
            z0 = product(split(jnp.concatenate([pick(re, 0), pick(im, 0)], axis=1)), tables[0], NT)
            z2 = product(split(jnp.concatenate([pick(re, 2), pick(im, 2)], axis=1)), tables[2], NT)
            both = jnp.concatenate(
                [
                    jnp.concatenate([pick(re, 1), pick(im, 1)], axis=1),
                    jnp.concatenate([pick(im, 1), -pick(re, 1)], axis=1),
                ],
                axis=0,
            )
            z1 = product(split(both), tables[1], NT)
            z1_re, z1_im = z1[:rows], z1[rows:]
            even, odd = z0 + z2, z0 - z2
            parts = (even + z1_re, odd - z1_im, even - z1_re, odd + z1_im)
            for t in range(RADIX):
                span = pl.ds(t * tile, tile)
                term = parts[t].reshape(PB, box_edge, tile) * moved_box[:, :, span]
                out[o, :, span] = out[o, :, span] - jnp.sum(term, axis=0)
            return carry

        lax.fori_loop(0, (filled + PB - 1) // PB, block, 0)
        summed = jnp.sum(out[o] * centre, axis=0, keepdims=True)
        total = total + jnp.sum(summed, axis=1, keepdims=True)
    energy[...] = total


def body(orbitals, corners, partners, kernel):
    own_count, box_edge, plane = orbitals.shape
    slab_count = lax.axis_size("slab")
    orb_count = lax.axis_size("orb")
    halo_depth = (ZDEV + box_edge - 2) // ZDEV
    rep_count = lax.axis_size("rep")
    turned = slab_count <= 2 * halo_depth + 1 and orb_count == rep_count
    if turned:
        pools = turned_boxes(orbitals)
    else:
        gathered = lax.all_gather(orbitals, "orb", axis=0, tiled=True)
        lower = [gathered]
        upper = [gathered]
        for _ in range(halo_depth):
            lower.append(passed_along(lower[-1], "slab", 1))
            upper.append(passed_along(upper[-1], "slab", -1))
        pools = [jnp.concatenate(lower[::-1] + upper[1:], axis=0)]
    cube = kernel.reshape(box_edge, box_edge, box_edge) * (1.0 / box_edge**3)
    mirrored = jnp.roll(jnp.flip(cube, (0, 1, 2)), 1, (0, 1, 2))
    filters = jnp.concatenate(
        [cube[:, 0::RADIX], cube[:, 1::RADIX] + mirrored[:, 1::RADIX], cube[:, 2::RADIX]], axis=1
    ).reshape(box_edge, (RADIX - 1) * plane // RADIX)
    plane_tab, edge_tab = fourier_tables(box_edge)
    smem = pl.BlockSpec(memory_space=pltpu.SMEM)
    vmem = pl.BlockSpec(memory_space=pltpu.VMEM)
    exchange, energy = pl.pallas_call(
        functools.partial(
            pair_kernel,
            slab_count=slab_count,
            orb_count=orb_count,
            rep_count=rep_count,
            halo_depth=halo_depth,
            turned=turned,
        ),
        in_specs=[smem, smem, vmem, vmem, vmem, vmem] + [vmem] * len(pools),
        out_specs=[vmem, vmem],
        out_shape=[
            jax.ShapeDtypeStruct((own_count, box_edge, plane), jnp.float32),
            jax.ShapeDtypeStruct((1, 1), jnp.float32),
        ],
        scratch_shapes=[
            pltpu.VMEM((PB, box_edge, plane), jnp.float32),
            pltpu.SMEM((partners.shape[1] + 1,), jnp.int32),
        ],
        name="pairs",
    )(partners, corners, orbitals, filters, plane_tab, edge_tab, *pools)
    exchange = swapped_sum(exchange, ("rep",))
    energy_all = swapped_sum(swapped_sum(energy.reshape(1), ("slab",)), ("orb", "rep"))
    orbital_total = own_count * slab_count * orb_count
    return exchange, energy_all / (2.0 * orbital_total * box_edge**3)


def solution(mesh):
    in_specs = (
        P(("grp", "slab", "orb"), None, None),
        P("grp", None),
        P(("grp", "slab", "orb"), None),
        P(),
    )
    out_specs = (P(("grp", "slab", "orb"), None, None), P("grp"))
    return jax.shard_map(body, mesh=mesh, in_specs=in_specs, out_specs=out_specs, check_vma=False)
```

profile of v0, /device:TPU:0, one launch (start us, length us, event | category | flops | bytes accessed | tf_op | source)
XLA Modules:
  0.0 41.7 jit_solution(873703081572190401)
XLA Ops:
  0.6 1.5 %collective-permute-start = (bf16[1,32,1024]{2,1,0:T(8,128)(2,1)}, bf16[1,32,1024]{2,1,0:T(8,128)(2,1)S(1)}, u32[]{:S(2)}, u32[]{:S(2)}) collective-permute-start(bf16[1,32,1024]{2,1,0:T(8,128)(2,1)} %refs_2_.1), channel_id=1, source_target_pairs={{0,0},{1,2},{2,1},{3,3},{4,4},{5,6},{6,5},{7,7},{8,8},{9,10},{10,9... | collective-permute-start | bytes 196616 | tf_op jit(solution)/shard_map/ppermute | solution.py:46
  2.1 3.1 %collective-permute-start.1 = (bf16[1,32,1024]{2,1,0:T(8,128)(2,1)}, bf16[1,32,1024]{2,1,0:T(8,128)(2,1)S(1)}, u32[]{:S(2)}, u32[]{:S(2)}) collective-permute-start(bf16[1,32,1024]{2,1,0:T(8,128)(2,1)} %refs_2_.1), channel_id=1, source_target_pairs={{0,4},{1,6},{2,5},{3,7},{4,8},{5,10},{6,9},{7,11},{8,12},{9,14},{1... | collective-permute-start | bytes 196616 | tf_op jit(solution)/shard_map/ppermute | solution.py:46
  5.2 2.6 %collective-permute-start.2 = (bf16[1,32,1024]{2,1,0:T(8,128)(2,1)}, bf16[1,32,1024]{2,1,0:T(8,128)(2,1)S(1)}, u32[]{:S(2)}, u32[]{:S(2)}) collective-permute-start(bf16[1,32,1024]{2,1,0:T(8,128)(2,1)} %refs_2_.1), channel_id=1, source_target_pairs={{0,8},{1,10},{2,9},{3,11},{4,12},{5,14},{6,13},{7,15},{8,0},{9,2},... | collective-permute-start | bytes 196616 | tf_op jit(solution)/shard_map/ppermute | solution.py:46
  7.8 1.3 %collective-permute-start.3 = (bf16[1,32,1024]{2,1,0:T(8,128)(2,1)}, bf16[1,32,1024]{2,1,0:T(8,128)(2,1)S(1)}, u32[]{:S(2)}, u32[]{:S(2)}) collective-permute-start(bf16[1,32,1024]{2,1,0:T(8,128)(2,1)} %refs_2_.1), channel_id=1, source_target_pairs={{0,12},{1,14},{2,13},{3,15},{4,0},{5,2},{6,1},{7,3},{8,4},{9,6},{1... | collective-permute-start | bytes 196616 | tf_op jit(solution)/shard_map/ppermute | solution.py:46
  9.1 1.1 %reshape.13 = f32[32,32,32]{2,1,0:T(8,128)S(1)} reshape(f32[32,1024]{1,0:T(8,128)} %param.9) | data formatting | bytes 262144 | tf_op jit(solution)/shard_map/reshape | solution.py:219
  10.2 0.2 reverse.3
  10.6 0.1 slice.37
  10.7 0.1 slice.36
  10.8 0.1 slice.45
  10.9 0.1 fusion
  11.0 0.2 slice.48
  11.2 0.0 copy-start.4
  11.2 0.2 pad_maximum_fusion.2
  11.4 0.1 slice.44
  11.6 0.8 %reshape.14.refs_3_ = f32[32,768]{1,0:T(8,128)} reshape(f32[32,24,32]{2,1,0:T(8,128)S(1)} %pad_maximum_fusion.3) | data formatting | bytes 196608 | tf_op jit(solution)/shard_map/reshape | solution.py:223
  12.4 0.0 copy-done.4
  12.4 0.7 %copy.8.refs_1_ = s32[8,3]{1,0:T(8,128)} copy(s32[8,3]{0,1:T(4,128)S(1)} %copy-done.4) | data formatting | bytes 192 | tf_op args[1]
  13.1 0.0 collective-permute-done.refs_6_
  13.1 0.0 copy-start
  13.1 0.0 collective-permute-done.1.refs_7_
  13.1 0.0 copy-start.1
  13.1 0.0 collective-permute-done.2.refs_8_
  13.1 0.0 copy-start.2
  13.1 0.0 collective-permute-done.3.refs_9_
  13.1 0.6 %copy-done = bf16[1,32,1024]{2,1,0:T(8,128)(2,1)} copy-done((bf16[1,32,1024]{2,1,0:T(8,128)(2,1)}, bf16[1,32,1024]{2,1,0:T(8,128)(2,1)S(1)}, u32[]{:S(2)}) %copy-start) | copy-done | bytes 65560
  13.7 0.0 copy-done.1
  13.7 0.0 copy-done.2
  13.8 0.0 copy-start.3
  13.8 0.6 %copy-done.3 = bf16[1,32,1024]{2,1,0:T(8,128)(2,1)} copy-done((bf16[1,32,1024]{2,1,0:T(8,128)(2,1)}, bf16[1,32,1024]{2,1,0:T(8,128)(2,1)S(1)}, u32[]{:S(2)}) %copy-start.3) | copy-done | bytes 65560
  14.4 5.8 %pairs.1 = (f32[1,32,1024]{2,1,0:T(8,128)}, f32[1,1]{1,0:T(1,128)}) custom-call(s32[1,24]{1,0:T(1,128)} %refs_0_.1, s32[8,3]{1,0:T(8,128)} %copy.8.refs_1_, bf16[1,32,1024]{2,1,0:T(8,128)(2,1)} %refs_2_.1, f32[32,768]{1,0:T(8,128)} %reshape.14.refs_3_, bf16[2,3,256,512]{3,2,1,0:T(8,128)(2,1)} %constant.9.clone.refs_4_, ...), custom_call_target="tpu_custom_call" | custom-call | tf_op jit(solution)/shard_map/pairs/pallas_call | solution.py:227
  20.2 2.2 %collective-permute-start.4 = (f32[1,32,1024]{2,1,0:T(8,128)}, f32[1,32,1024]{2,1,0:T(8,128)S(1)}, u32[]{:S(2)}, u32[]{:S(2)}) collective-permute-start(f32[1,32,1024]{2,1,0:T(8,128)} %get-tuple-element.4), channel_id=1, source_target_pairs={{0,1},{1,0},{2,3},{3,2},{4,5},{5,4},{6,7},{7,6},{8,9},{9,8},{10,11... | collective-permute-start | bytes 393224 | tf_op jit(solution)/shard_map/ppermute | solution.py:28
  22.3 0.0 collective-permute-start.6
  22.3 3.0 %collective-permute-start.7 = (f32[1]{0:T(128)}, f32[1]{0:T(128)}, u32[]{:S(2)}, u32[]{:S(2)}) collective-permute-start(f32[1]{0:T(128)} %bitcast), channel_id=1, source_target_pairs={{0,12},{4,8},{8,4},{12,0},{1,13},{5,9},{9,5},{13,1},{2,14},{6,10},... | collective-permute-start | bytes 20 | tf_op jit(solution)/shard_map/ppermute | solution.py:28
  25.3 0.5 %collective-permute-start.5 = (f32[1]{0:T(128)}, f32[1]{0:T(128)}, u32[]{:S(2)}, u32[]{:S(2)}) collective-permute-start(f32[1]{0:T(128)} %bitcast), channel_id=1, source_target_pairs={{0,4},{4,0},{8,12},{12,8},{1,5},{5,1},{9,13},{13,9},{2,6},{6,2},{1... | collective-permute-start | bytes 20 | tf_op jit(solution)/shard_map/ppermute | solution.py:28
  25.8 3.2 %collective-permute-done.5 = f32[1]{0:T(128)} collective-permute-done((f32[1]{0:T(128)}, f32[1]{0:T(128)}, u32[]{:S(2)}, u32[]{:S(2)}) %collective-permute-start.5) | collective-permute-done | bytes 36 | tf_op jit(solution)/shard_map/ppermute | solution.py:28
  30.3 0.0 collective-permute-done.6
  30.3 0.0 collective-permute-done.7
  31.5 1.5 %collective-permute-start.10 = (f32[1]{0:T(128)}, f32[1]{0:T(128)}, u32[]{:S(2)}, u32[]{:S(2)}) collective-permute-start(f32[1]{0:T(128)} %add.28), channel_id=1, source_target_pairs={{0,3},{1,2},{2,1},{3,0},{4,7},{5,6},{6,5},{7,4},{8,11},{9,10},{10,... | collective-permute-start | bytes 20 | tf_op jit(solution)/shard_map/ppermute | solution.py:28
  33.1 2.8 %collective-permute-start.9 = (f32[1]{0:T(128)}, f32[1]{0:T(128)}, u32[]{:S(2)}, u32[]{:S(2)}) collective-permute-start(f32[1]{0:T(128)} %add.28), channel_id=1, source_target_pairs={{0,2},{1,3},{2,0},{3,1},{4,6},{5,7},{6,4},{7,5},{8,10},{9,11},{10,... | collective-permute-start | bytes 20 | tf_op jit(solution)/shard_map/ppermute | solution.py:28
  35.9 0.8 %collective-permute-start.8 = (f32[1]{0:T(128)}, f32[1]{0:T(128)}, u32[]{:S(2)}, u32[]{:S(2)}) collective-permute-start(f32[1]{0:T(128)} %add.28), channel_id=1, source_target_pairs={{0,1},{1,0},{2,3},{3,2},{4,5},{5,4},{6,7},{7,6},{8,9},{9,8},{10,11... | collective-permute-start | bytes 20 | tf_op jit(solution)/shard_map/ppermute | solution.py:28
  36.7 0.3 collective-permute-done.8
  37.7 0.0 collective-permute-done.10
  37.7 0.0 collective-permute-done.9
  38.9 0.0 collective-permute-done.4
  38.9 1.6 %add.25 = f32[1,32,1024]{2,1,0:T(8,128)} add(f32[1,32,1024]{2,1,0:T(8,128)} %get-tuple-element.4, f32[1,32,1024]{2,1,0:T(8,128)S(1)} %collective-permute-done.4) | non-fusion elementwise | flops 32768 | bytes 393216 | tf_op jit(solution)/shard_map/add | solution.py:31
  (6 shorter events, 0.2 us)
Async XLA Ops:
  0.6 12.5 %collective-permute-start = (bf16[1,32,1024]{2,1,0:T(8,128)(2,1)}, bf16[1,32,1024]{2,1,0:T(8,128)(2,1)S(1)}, u32[]{:S(2)}, u32[]{:S(2)}) collective-permute-start(bf16[1,32,1024]{2,1,0:T(8,128)(2,1)} %refs_2_.1), channel_id=1, source_target_pairs={{0,0},{1,2},{2,1},{3,3},{4,4},{5,6},{6,5},{7,7},{8,8},{9,10},{10,9... | collective-permute-start | bytes 196616 | tf_op jit(solution)/shard_map/ppermute | solution.py:46
  2.1 11.0 %collective-permute-start.1 = (bf16[1,32,1024]{2,1,0:T(8,128)(2,1)}, bf16[1,32,1024]{2,1,0:T(8,128)(2,1)S(1)}, u32[]{:S(2)}, u32[]{:S(2)}) collective-permute-start(bf16[1,32,1024]{2,1,0:T(8,128)(2,1)} %refs_2_.1), channel_id=1, source_target_pairs={{0,4},{1,6},{2,5},{3,7},{4,8},{5,10},{6,9},{7,11},{8,12},{9,14},{1... | collective-permute-start | bytes 196616 | tf_op jit(solution)/shard_map/ppermute | solution.py:46
  5.2 7.9 %collective-permute-start.2 = (bf16[1,32,1024]{2,1,0:T(8,128)(2,1)}, bf16[1,32,1024]{2,1,0:T(8,128)(2,1)S(1)}, u32[]{:S(2)}, u32[]{:S(2)}) collective-permute-start(bf16[1,32,1024]{2,1,0:T(8,128)(2,1)} %refs_2_.1), channel_id=1, source_target_pairs={{0,8},{1,10},{2,9},{3,11},{4,12},{5,14},{6,13},{7,15},{8,0},{9,2},... | collective-permute-start | bytes 196616 | tf_op jit(solution)/shard_map/ppermute | solution.py:46
  7.8 5.4 %collective-permute-start.3 = (bf16[1,32,1024]{2,1,0:T(8,128)(2,1)}, bf16[1,32,1024]{2,1,0:T(8,128)(2,1)S(1)}, u32[]{:S(2)}, u32[]{:S(2)}) collective-permute-start(bf16[1,32,1024]{2,1,0:T(8,128)(2,1)} %refs_2_.1), channel_id=1, source_target_pairs={{0,12},{1,14},{2,13},{3,15},{4,0},{5,2},{6,1},{7,3},{8,4},{9,6},{1... | collective-permute-start | bytes 196616 | tf_op jit(solution)/shard_map/ppermute | solution.py:46
  11.2 1.2 %copy-start.4 = (s32[8,3]{0,1:T(4,128)S(1)}, s32[8,3]{0,1:T(4,128)}, u32[]{:S(2)}) copy-start(s32[8,3]{0,1:T(4,128)} %param.7) | copy-start | bytes 292
  13.1 0.6 %copy-start = (bf16[1,32,1024]{2,1,0:T(8,128)(2,1)}, bf16[1,32,1024]{2,1,0:T(8,128)(2,1)S(1)}, u32[]{:S(2)}) copy-start(bf16[1,32,1024]{2,1,0:T(8,128)(2,1)S(1)} %collective-permute-done.refs_6_) | copy-start | bytes 196612
  13.1 0.6 %copy-start.1 = (bf16[1,32,1024]{2,1,0:T(8,128)(2,1)}, bf16[1,32,1024]{2,1,0:T(8,128)(2,1)S(1)}, u32[]{:S(2)}) copy-start(bf16[1,32,1024]{2,1,0:T(8,128)(2,1)S(1)} %collective-permute-done.1.refs_7_) | copy-start | bytes 196612
  13.1 0.6 %copy-start.2 = (bf16[1,32,1024]{2,1,0:T(8,128)(2,1)}, bf16[1,32,1024]{2,1,0:T(8,128)(2,1)S(1)}, u32[]{:S(2)}) copy-start(bf16[1,32,1024]{2,1,0:T(8,128)(2,1)S(1)} %collective-permute-done.2.refs_8_) | copy-start | bytes 196612
  13.8 0.6 %copy-start.3 = (bf16[1,32,1024]{2,1,0:T(8,128)(2,1)}, bf16[1,32,1024]{2,1,0:T(8,128)(2,1)S(1)}, u32[]{:S(2)}) copy-start(bf16[1,32,1024]{2,1,0:T(8,128)(2,1)S(1)} %collective-permute-done.3.refs_9_) | copy-start | bytes 196612
  20.2 18.8 %collective-permute-start.4 = (f32[1,32,1024]{2,1,0:T(8,128)}, f32[1,32,1024]{2,1,0:T(8,128)S(1)}, u32[]{:S(2)}, u32[]{:S(2)}) collective-permute-start(f32[1,32,1024]{2,1,0:T(8,128)} %get-tuple-element.4), channel_id=1, source_target_pairs={{0,1},{1,0},{2,3},{3,2},{4,5},{5,4},{6,7},{7,6},{8,9},{9,8},{10,11... | collective-permute-start | bytes 393224 | tf_op jit(solution)/shard_map/ppermute | solution.py:28
  22.3 8.0 %collective-permute-start.6 = (f32[1]{0:T(128)}, f32[1]{0:T(128)}, u32[]{:S(2)}, u32[]{:S(2)}) collective-permute-start(f32[1]{0:T(128)} %bitcast), channel_id=1, source_target_pairs={{0,8},{4,12},{8,0},{12,4},{1,9},{5,13},{9,1},{13,5},{2,10},{6,14},... | collective-permute-start | bytes 20 | tf_op jit(solution)/shard_map/ppermute | solution.py:28
  22.3 8.0 %collective-permute-start.7 = (f32[1]{0:T(128)}, f32[1]{0:T(128)}, u32[]{:S(2)}, u32[]{:S(2)}) collective-permute-start(f32[1]{0:T(128)} %bitcast), channel_id=1, source_target_pairs={{0,12},{4,8},{8,4},{12,0},{1,13},{5,9},{9,5},{13,1},{2,14},{6,10},... | collective-permute-start | bytes 20 | tf_op jit(solution)/shard_map/ppermute | solution.py:28
  25.3 3.7 %collective-permute-start.5 = (f32[1]{0:T(128)}, f32[1]{0:T(128)}, u32[]{:S(2)}, u32[]{:S(2)}) collective-permute-start(f32[1]{0:T(128)} %bitcast), channel_id=1, source_target_pairs={{0,4},{4,0},{8,12},{12,8},{1,5},{5,1},{9,13},{13,9},{2,6},{6,2},{1... | collective-permute-start | bytes 20 | tf_op jit(solution)/shard_map/ppermute | solution.py:28
  31.5 6.2 %collective-permute-start.10 = (f32[1]{0:T(128)}, f32[1]{0:T(128)}, u32[]{:S(2)}, u32[]{:S(2)}) collective-permute-start(f32[1]{0:T(128)} %add.28), channel_id=1, source_target_pairs={{0,3},{1,2},{2,1},{3,0},{4,7},{5,6},{6,5},{7,4},{8,11},{9,10},{10,... | collective-permute-start | bytes 20 | tf_op jit(solution)/shard_map/ppermute | solution.py:28
  33.1 4.7 %collective-permute-start.9 = (f32[1]{0:T(128)}, f32[1]{0:T(128)}, u32[]{:S(2)}, u32[]{:S(2)}) collective-permute-start(f32[1]{0:T(128)} %add.28), channel_id=1, source_target_pairs={{0,2},{1,3},{2,0},{3,1},{4,6},{5,7},{6,4},{7,5},{8,10},{9,11},{10,... | collective-permute-start | bytes 20 | tf_op jit(solution)/shard_map/ppermute | solution.py:28
  35.9 1.1 %collective-permute-start.8 = (f32[1]{0:T(128)}, f32[1]{0:T(128)}, u32[]{:S(2)}, u32[]{:S(2)}) collective-permute-start(f32[1]{0:T(128)} %add.28), channel_id=1, source_target_pairs={{0,1},{1,0},{2,3},{3,2},{4,5},{5,4},{6,7},{7,6},{8,9},{9,8},{10,11... | collective-permute-start | bytes 20 | tf_op jit(solution)/shard_map/ppermute | solution.py:28
where the time goes:
time: 42 us; the launch traced here: 41.7 us
  starting transfers between devices  19.3 us (46%)
  between operations  6.35 us (15%)
  Pallas kernels  5.76 us (14%)
  local copies, waits for them, and re-layouts  4.7 us (11%)
  waiting for transfers between devices  3.54 us (8%)
  other arithmetic  1.99 us (5%)
    ppermute x7, starting transfers between devices, swapped_sum(): lax.ppermute(value, axes, [(i, i ^ d) for i in range(size)])  10.8 us
    ppermute x4, starting transfers between devices, turned_boxes(): boxes.append(lax.ppermute(orbitals, axes, moves))  8.49 us
    pallas_call x1, Pallas kernels, body(): pl.pallas_call(functools.partial(pair_kernel, slab_count=slab_count, orb_...  5.76 us
    ppermute x7, waiting for transfers between devices, swapped_sum(): lax.ppermute(value, axes, [(i, i ^ d) for i in range(size)])  3.53 us
    unnamed x11, local copies, waits for them, and re-layouts  1.92 us
    add x1, other arithmetic, swapped_sum(): terms = [terms[i] + terms[i + 1] for i in range(0, len(terms), 2)]  1.58 us
    reshape x1, local copies, waits for them, and re-layouts, body(): cube = kernel.reshape(box_edge, box_edge, box_edge) * (1.0 / box_edge ** 3)  1.07 us
  transfers between devices with their start and end apart: 11, of which 2 were waited for; matrix products, arithmetic and copies ran while one was open for 9% of the time, Pallas kernels for 0%

commit v1 on v0

--- a/solution.py
+++ b/solution.py
@@ -21,15 +21,16 @@
 
 
 def swapped_sum(value, axes):
-    size = math.prod(lax.axis_size(axis) for axis in axes)
-    if size & (size - 1) or size > 4:
-        return lax.psum(value, axes)
-    terms = [value] + [
-        lax.ppermute(value, axes, [(i, i ^ d) for i in range(size)]) for d in range(1, size)
-    ]
-    while len(terms) > 1:
-        terms = [terms[i] + terms[i + 1] for i in range(0, len(terms), 2)]
-    return terms[0]
+    for axis in axes:
+        size = lax.axis_size(axis)
+        if size & (size - 1):
+            value = lax.psum(value, axis)
+            continue
+        step = 1
+        while step < size:
+            value = value + lax.ppermute(value, axis, [(i, i ^ step) for i in range(size)])
+            step *= 2
+    return value
 
 
 def turned_boxes(orbitals):
@@ -89,10 +90,57 @@
 NT = ((1,), (1,))
 
 
+def one_hot(source, target):
+    return (source == target).astype(jnp.float32).astype(jnp.bfloat16)
+
+
+def moved_by(left, right):
+    return jnp.dot(left, right, preferred_element_type=jnp.float32)
+
+
+def ordered_filters(kernel):
+    box_edge, plane = kernel.shape
+    tile, inner = plane // RADIX, box_edge // RADIX
+    high, rest = split(kernel)
+    rest = kernel - high.astype(jnp.float32)
+    mid, low = split(rest)
+    pieces = jnp.concatenate([high, mid, low], axis=0)
+    count = pieces.shape[0]
+    stacked = jnp.concatenate([pieces[:, t * tile:(t + 1) * tile] for t in range(RADIX)], axis=0)
+    source = lax.broadcasted_iota(jnp.int32, (tile, tile), 0)
+    target = lax.broadcasted_iota(jnp.int32, (tile, tile), 1)
+    share = tile // RADIX
+    within = target % share
+    decimated = (target // share + RADIX * (within // box_edge)) * box_edge + within % box_edge
+    stacked = moved_by(stacked, one_hot(source, decimated))
+    groups = [
+        jnp.concatenate(
+            [
+                stacked[t * count:(t + 1) * count, q * share:(q + 1) * share]
+                for t in range(RADIX)
+            ],
+            axis=1,
+        )
+        for q in range(RADIX)
+    ]
+    back = (inner - 1 - target // box_edge) * box_edge + (box_edge - target % box_edge) % box_edge
+    mirrored = moved_by(groups[3].astype(jnp.bfloat16), one_hot(source, back))
+    rows = lax.broadcasted_iota(jnp.int32, (count, count), 0)
+    cols = lax.broadcasted_iota(jnp.int32, (count, count), 1)
+    opposite = rows // box_edge * box_edge + (box_edge - rows % box_edge) % box_edge
+    mirrored = moved_by(one_hot(opposite, cols), mirrored.astype(jnp.bfloat16))
+
+    def joined(group):
+        return group[:box_edge] + group[box_edge:2 * box_edge] + group[2 * box_edge:]
+
+    parts = [joined(groups[0]), joined(groups[1]) + joined(mirrored), joined(groups[2])]
+    return jnp.concatenate(parts, axis=1) * (1.0 / box_edge**3)
+
+
 def pair_kernel(*refs, slab_count, orb_count, rep_count, halo_depth, turned):
-    partners, corners, own, filters, plane_tab, edge_tab = refs[:6]
+    partners, corners, own, kernel, plane_tab, edge_tab = refs[:6]
     pools = refs[6:-4]
-    out, energy, moved_box, chosen = refs[-4:]
+    out, moved_box, filters, chosen = refs[-4:]
     own_count, box_edge, plane = own.shape
     slot_count = partners.shape[1]
     tile = plane // RADIX
@@ -106,6 +154,7 @@
     b_ids = lane_ids // box_edge
     c_ids = lane_ids % box_edge
     total = jnp.zeros((1, 1), jnp.float32)
+    filters[...] = ordered_filters(kernel[...])
     for o in range(own_count):
         centre = own[o].astype(jnp.float32)
         filled = jnp.int32(0)
@@ -115,7 +164,8 @@
             mine = (partner >= 0) & (lax.rem(column, rep_count) == lax.axis_index("rep"))
             chosen[filled] = partner
             filled = filled + mine.astype(jnp.int32)
-        out[o] = jnp.zeros((box_edge, plane), jnp.float32)
+        held = pl.ds(o * box_edge, box_edge)
+        out[held] = jnp.zeros((box_edge, plane), jnp.float32)
 
         def block(step, carry):
             for p in range(PB):
@@ -125,7 +175,7 @@
                 shift = []
                 for d in range(3):
                     half = lengths[d] // 2
-                    delta = corners[first_own + o, d] - corners[partner, d] + half
+                    delta = corners[d, first_own + o] - corners[d, partner] + half
                     delta = jnp.where(delta < 0, delta + lengths[d], delta)
                     delta = jnp.where(delta >= lengths[d], delta - lengths[d], delta)
                     shift.append(delta - half)
@@ -190,13 +240,13 @@
             for t in range(RADIX):
                 span = pl.ds(t * tile, tile)
                 term = parts[t].reshape(PB, box_edge, tile) * moved_box[:, :, span]
-                out[o, :, span] = out[o, :, span] - jnp.sum(term, axis=0)
+                out[held, span] = out[held, span] - jnp.sum(term, axis=0)
             return carry
 
         lax.fori_loop(0, (filled + PB - 1) // PB, block, 0)
-        summed = jnp.sum(out[o] * centre, axis=0, keepdims=True)
+        summed = jnp.sum(out[held] * centre, axis=0, keepdims=True)
         total = total + jnp.sum(summed, axis=1, keepdims=True)
-    energy[...] = total
+    out[pl.ds(own_count * box_edge, 8)] = jnp.broadcast_to(total, (8, plane))
 
 
 def body(orbitals, corners, partners, kernel):
@@ -216,15 +266,10 @@
             lower.append(passed_along(lower[-1], "slab", 1))
             upper.append(passed_along(upper[-1], "slab", -1))
         pools = [jnp.concatenate(lower[::-1] + upper[1:], axis=0)]
-    cube = kernel.reshape(box_edge, box_edge, box_edge) * (1.0 / box_edge**3)
-    mirrored = jnp.roll(jnp.flip(cube, (0, 1, 2)), 1, (0, 1, 2))
-    filters = jnp.concatenate(
-        [cube[:, 0::RADIX], cube[:, 1::RADIX] + mirrored[:, 1::RADIX], cube[:, 2::RADIX]], axis=1
-    ).reshape(box_edge, (RADIX - 1) * plane // RADIX)
     plane_tab, edge_tab = fourier_tables(box_edge)
     smem = pl.BlockSpec(memory_space=pltpu.SMEM)
     vmem = pl.BlockSpec(memory_space=pltpu.VMEM)
-    exchange, energy = pl.pallas_call(
+    sums = pl.pallas_call(
         functools.partial(
             pair_kernel,
             slab_count=slab_count,
@@ -234,19 +279,20 @@
             turned=turned,
         ),
         in_specs=[smem, smem, vmem, vmem, vmem, vmem] + [vmem] * len(pools),
-        out_specs=[vmem, vmem],
-        out_shape=[
-            jax.ShapeDtypeStruct((own_count, box_edge, plane), jnp.float32),
-            jax.ShapeDtypeStruct((1, 1), jnp.float32),
-        ],
+        out_specs=vmem,
+        out_shape=jax.ShapeDtypeStruct((own_count * box_edge + 8, plane), jnp.float32),
         scratch_shapes=[
             pltpu.VMEM((PB, box_edge, plane), jnp.float32),
+            pltpu.VMEM((box_edge, (RADIX - 1) * plane // RADIX), jnp.float32),
             pltpu.SMEM((partners.shape[1] + 1,), jnp.int32),
         ],
         name="pairs",
-    )(partners, corners, orbitals, filters, plane_tab, edge_tab, *pools)
-    exchange = swapped_sum(exchange, ("rep",))
-    energy_all = swapped_sum(swapped_sum(energy.reshape(1), ("slab",)), ("orb", "rep"))
+    )(partners, corners.T, orbitals, kernel, plane_tab, edge_tab, *pools)
+    held = own_count * box_edge
+    other = lax.ppermute(sums, "rep", [(i, i ^ 1) for i in range(rep_count)])
+    energy = sums[held:, :128] + other[held:, :128]
+    exchange = (sums[:held] + other[:held]).reshape(own_count, box_edge, plane)
+    energy_all = swapped_sum(energy, ("orb", "slab"))[0, :1]
     orbital_total = own_count * slab_count * orb_count
     return exchange, energy_all / (2.0 * orbital_total * box_edge**3)
 

time: 42 us -> 38.4 us (0.914)
  waiting for transfers between devices: 3.54 us -> 12.9 us
  starting transfers between devices: 19.3 us -> 13.1 us
  between operations: 6.35 us -> 2.43 us
  local copies, waits for them, and re-layouts: 4.7 us -> 1.13 us
  Pallas kernels: 5.76 us -> 6.33 us
    ppermute x7 -> x4, starting transfers between devices: 10.8 us -> 4.65 us  [the longest x1 2.42 us: body(): other = lax.ppermute(sums, 'rep', [(i, i ^ 1) for i in range(rep_count)])]
    ppermute x7 -> x4, waiting for transfers between devices: 3.53 us -> 9.15 us  [the longest x3 7.91 us: swapped_sum(): lax.ppermute(value, axis, [(i, i ^ step) for i in range(size)])]
    ppermute x4, waiting for transfers between devices: 0.01 us -> 3.72 us  [turned_boxes(): boxes.append(lax.ppermute(orbitals, axes, moves))]
    reshape x2 -> x0, local copies, waits for them, and re-layouts: 1.86 us -> none  [the longest x1 1.07 us: body(): cube = kernel.reshape(box_edge, box_edge, box_edge) * (1.0 / box_edge ** 3)]
    reshape x0 -> x1, other arithmetic: none -> 1.58 us  [body(): exchange = (sums[:held] + other[:held]).reshape(own_count, box_edge, plane)]
    unnamed x11 -> x8, local copies, waits for them, and re-layouts: 1.92 us -> 0.61 us
    add x2 -> x4, other arithmetic: 1.6 us -> 0.69 us  [the longest x1 0.68 us: body(): energy = sums[held:, :128] + other[held:, :128]]
    pallas_call x1, Pallas kernels: 5.76 us -> 6.33 us  [body(): pl.pallas_call(functools.partial(pair_kernel, slab_count=slab_count, orb_...]
  transfers between devices with their start and end apart: 11 -> 8, of which waited for: 2 -> 7; matrix products, arithmetic and copies ran while one was open for 9% -> 4% of each run, Pallas kernels for 0% -> 0%
where the time goes in v1:
time: 38.4 us; the launch traced here: 38.2 us
  starting transfers between devices  13.1 us (34%)
  waiting for transfers between devices  12.9 us (34%)
  Pallas kernels  6.33 us (16%)
  between operations  2.43 us (6%)
  other arithmetic  2.27 us (6%)
  local copies, waits for them, and re-layouts  1.13 us (3%)
    ppermute x4, starting transfers between devices, turned_boxes(): boxes.append(lax.ppermute(orbitals, axes, moves))  8.49 us
    ppermute x3, waiting for transfers between devices, swapped_sum(): lax.ppermute(value, axis, [(i, i ^ step) for i in range(size)])  7.91 us
    pallas_call x1, Pallas kernels, body(): pl.pallas_call(functools.partial(pair_kernel, slab_count=slab_count, orb_...  6.33 us
    ppermute x4, waiting for transfers between devices, turned_boxes(): boxes.append(lax.ppermute(orbitals, axes, moves))  3.72 us
    ppermute x1, starting transfers between devices, body(): other = lax.ppermute(sums, 'rep', [(i, i ^ 1) for i in range(rep_count)])  2.42 us
    ppermute x3, starting transfers between devices, swapped_sum(): lax.ppermute(value, axis, [(i, i ^ step) for i in range(size)])  2.23 us
    reshape x1, other arithmetic, body(): exchange = (sums[:held] + other[:held]).reshape(own_count, box_edge, plane)  1.58 us
    ppermute x1, waiting for transfers between devices, body(): other = lax.ppermute(sums, 'rep', [(i, i ^ 1) for i in range(rep_count)])  1.24 us
  transfers between devices with their start and end apart: 8, of which 7 were waited for; matrix products, arithmetic and copies ran while one was open for 4% of the time, Pallas kernels for 0%

profile of v1, /device:TPU:0, one launch (start us, length us, event | category | flops | bytes accessed | tf_op | source)
XLA Modules:
  0.0 38.2 jit_solution(209503954135759200)
XLA Ops:
  0.6 1.5 %collective-permute-start = (bf16[1,32,1024]{2,1,0:T(8,128)(2,1)}, bf16[1,32,1024]{2,1,0:T(8,128)(2,1)S(1)}, u32[]{:S(2)}, u32[]{:S(2)}) collective-permute-start(bf16[1,32,1024]{2,1,0:T(8,128)(2,1)} %refs_2_.1), channel_id=1, source_target_pairs={{0,0},{1,2},{2,1},{3,3},{4,4},{5,6},{6,5},{7,7},{8,8},{9,10},{10,9... | collective-permute-start | bytes 196616 | tf_op jit(solution)/shard_map/ppermute | solution.py:47
  2.1 3.1 %collective-permute-start.1 = (bf16[1,32,1024]{2,1,0:T(8,128)(2,1)}, bf16[1,32,1024]{2,1,0:T(8,128)(2,1)S(1)}, u32[]{:S(2)}, u32[]{:S(2)}) collective-permute-start(bf16[1,32,1024]{2,1,0:T(8,128)(2,1)} %refs_2_.1), channel_id=1, source_target_pairs={{0,4},{1,6},{2,5},{3,7},{4,8},{5,10},{6,9},{7,11},{8,12},{9,14},{1... | collective-permute-start | bytes 196616 | tf_op jit(solution)/shard_map/ppermute | solution.py:47
  5.2 2.6 %collective-permute-start.2 = (bf16[1,32,1024]{2,1,0:T(8,128)(2,1)}, bf16[1,32,1024]{2,1,0:T(8,128)(2,1)S(1)}, u32[]{:S(2)}, u32[]{:S(2)}) collective-permute-start(bf16[1,32,1024]{2,1,0:T(8,128)(2,1)} %refs_2_.1), channel_id=1, source_target_pairs={{0,8},{1,10},{2,9},{3,11},{4,12},{5,14},{6,13},{7,15},{8,0},{9,2},... | collective-permute-start | bytes 196616 | tf_op jit(solution)/shard_map/ppermute | solution.py:47
  7.8 1.3 %collective-permute-start.3 = (bf16[1,32,1024]{2,1,0:T(8,128)(2,1)}, bf16[1,32,1024]{2,1,0:T(8,128)(2,1)S(1)}, u32[]{:S(2)}, u32[]{:S(2)}) collective-permute-start(bf16[1,32,1024]{2,1,0:T(8,128)(2,1)} %refs_2_.1), channel_id=1, source_target_pairs={{0,12},{1,14},{2,13},{3,15},{4,0},{5,2},{6,1},{7,3},{8,4},{9,6},{1... | collective-permute-start | bytes 196616 | tf_op jit(solution)/shard_map/ppermute | solution.py:47
  9.1 0.0 collective-permute-done.refs_6_
  9.1 0.0 copy-start
  9.1 0.5 %collective-permute-done.1.refs_7_ = bf16[1,32,1024]{2,1,0:T(8,128)(2,1)S(1)} collective-permute-done((bf16[1,32,1024]{2,1,0:T(8,128)(2,1)}, bf16[1,32,1024]{2,1,0:T(8,128)(2,1)S(1)}, u32[]{:S(2)}, u32[]{:S(2)}) %collective-permute-start.1) | collective-permute-done | bytes 65568 | tf_op jit(solution)/shard_map/ppermute | solution.py:47
  9.7 0.0 copy-start.1
  9.7 2.5 %collective-permute-done.2.refs_8_ = bf16[1,32,1024]{2,1,0:T(8,128)(2,1)S(1)} collective-permute-done((bf16[1,32,1024]{2,1,0:T(8,128)(2,1)}, bf16[1,32,1024]{2,1,0:T(8,128)(2,1)S(1)}, u32[]{:S(2)}, u32[]{:S(2)}) %collective-permute-start.2) | collective-permute-done | bytes 65568 | tf_op jit(solution)/shard_map/ppermute | solution.py:47
  12.2 0.0 copy-start.2
  12.2 0.7 %collective-permute-done.3.refs_9_ = bf16[1,32,1024]{2,1,0:T(8,128)(2,1)S(1)} collective-permute-done((bf16[1,32,1024]{2,1,0:T(8,128)(2,1)}, bf16[1,32,1024]{2,1,0:T(8,128)(2,1)S(1)}, u32[]{:S(2)}, u32[]{:S(2)}) %collective-permute-start.3) | collective-permute-done | bytes 65568 | tf_op jit(solution)/shard_map/ppermute | solution.py:47
  12.8 0.0 copy-start.3
  12.9 0.0 copy-done
  12.9 0.0 copy-done.1
  12.9 0.0 copy-done.2
  12.9 0.6 %copy-done.3 = bf16[1,32,1024]{2,1,0:T(8,128)(2,1)} copy-done((bf16[1,32,1024]{2,1,0:T(8,128)(2,1)}, bf16[1,32,1024]{2,1,0:T(8,128)(2,1)S(1)}, u32[]{:S(2)}) %copy-start.3) | copy-done | bytes 65560
  13.5 6.3 %pairs.1 = f32[40,1024]{1,0:T(8,128)} custom-call(s32[1,24]{1,0:T(1,128)} %refs_0_.1, s32[3,8]{1,0:T(4,128)} %bitcast.4, bf16[1,32,1024]{2,1,0:T(8,128)(2,1)} %refs_2_.1, f32[32,1024]{1,0:T(8,128)} %refs_3_.1, bf16[2,3,256,512]{3,2,1,0:T(8,128)(2,1)} %constant.8.clone.refs_4_, bf16[2,2,256,256]{3,2,1,0:T(8,128)(2,1)} %constant.9.clone.refs_5_, ...), custom_call_target="tpu_custom_call" | custom-call | tf_op jit(solution)/shard_map/pairs/pallas_call | solution.py:272
  19.8 2.4 %collective-permute-start.4 = (f32[40,1024]{1,0:T(8,128)}, f32[40,1024]{1,0:T(8,128)S(1)}, u32[]{:S(2)}, u32[]{:S(2)}) collective-permute-start(f32[40,1024]{1,0:T(8,128)} %pairs.1), channel_id=1, source_target_pairs={{0,1},{1,0},{2,3},{3,2},{4,5},{5,4},{6,7},{7,6},{8,9},{9,8},{10,11... | collective-permute-start | bytes 491528 | tf_op jit(solution)/shard_map/ppermute | solution.py:292
  22.2 1.2 %collective-permute-done.4 = f32[40,1024]{1,0:T(8,128)S(1)} collective-permute-done((f32[40,1024]{1,0:T(8,128)}, f32[40,1024]{1,0:T(8,128)S(1)}, u32[]{:S(2)}, u32[]{:S(2)}) %collective-permute-start.4) | collective-permute-done | bytes 163872 | tf_op jit(solution)/shard_map/ppermute | solution.py:292
  23.5 0.7 %slice_add_fusion.1 = f32[8,128]{1,0:T(8,128)S(1)} fusion(f32[40,1024]{1,0:T(8,128)S(1)} %collective-permute-done.4, f32[40,1024]{1,0:T(8,128)} %pairs.1), kind=kLoop, calls=%fused_computation.2 | loop fusion | flops 1024 | bytes 12288 | tf_op jit(solution)/shard_map/add | solution.py:293
  24.1 0.5 %collective-permute-start.5 = (f32[8,128]{1,0:T(8,128)S(1)}, f32[8,128]{1,0:T(8,128)S(1)}, u32[]{:S(2)}, u32[]{:S(2)}) collective-permute-start(f32[8,128]{1,0:T(8,128)S(1)} %slice_add_fusion.1), channel_id=1, source_target_pairs={{0,2},{2,0},{1,3},{3,1},{4,6},{6,4},{5,7},{7,5},{8,10},{10,8},{9,1... | collective-permute-start | bytes 12296 | tf_op jit(solution)/shard_map/ppermute | solution.py:31
  24.7 3.1 %collective-permute-done.5 = f32[8,128]{1,0:T(8,128)S(1)} collective-permute-done((f32[8,128]{1,0:T(8,128)S(1)}, f32[8,128]{1,0:T(8,128)S(1)}, u32[]{:S(2)}, u32[]{:S(2)}) %collective-permute-start.5) | collective-permute-done | bytes 4128 | tf_op jit(solution)/shard_map/ppermute | solution.py:31
  27.7 0.0 collective-permute-start.6
  27.8 3.6 %collective-permute-done.6 = f32[8,128]{1,0:T(8,128)S(1)} collective-permute-done((f32[8,128]{1,0:T(8,128)S(1)}, f32[8,128]{1,0:T(8,128)S(1)}, u32[]{:S(2)}, u32[]{:S(2)}) %collective-permute-start.6) | collective-permute-done | bytes 4128 | tf_op jit(solution)/shard_map/ppermute | solution.py:31
  31.4 1.7 %collective-permute-start.7 = (f32[8,128]{1,0:T(8,128)S(1)}, f32[8,128]{1,0:T(8,128)S(1)}, u32[]{:S(2)}, u32[]{:S(2)}) collective-permute-start(f32[8,128]{1,0:T(8,128)S(1)} %add.18), channel_id=1, source_target_pairs={{0,8},{4,12},{8,0},{12,4},{1,9},{5,13},{9,1},{13,5},{2,10},{6,14},... | collective-permute-start | bytes 12296 | tf_op jit(solution)/shard_map/ppermute | solution.py:31
  33.0 1.6 %fusion = f32[1,32,1024]{2,1,0:T(8,128)} fusion(f32[40,1024]{1,0:T(8,128)S(1)} %collective-permute-done.4, f32[40,1024]{1,0:T(8,128)} %pairs.1), kind=kLoop, calls=%fused_computation.1 | loop fusion | flops 32768 | bytes 393216 | tf_op jit(solution)/shard_map/reshape | solution.py:294
  34.6 1.2 %collective-permute-done.7 = f32[8,128]{1,0:T(8,128)S(1)} collective-permute-done((f32[8,128]{1,0:T(8,128)S(1)}, f32[8,128]{1,0:T(8,128)S(1)}, u32[]{:S(2)}, u32[]{:S(2)}) %collective-permute-start.7) | collective-permute-done | bytes 4128 | tf_op jit(solution)/shard_map/ppermute | solution.py:31
  35.9 0.5 %slice.19 = f32[1,1]{1,0:T(1,128)} slice(f32[8,128]{1,0:T(8,128)S(1)} %add.19), slice={[0:1], [0:1]} | slice | bytes 8 | tf_op jit(solution)/shard_map/slice | solution.py:295
  (3 shorter events, 0.0 us)
Async XLA Ops:
  0.6 8.5 %collective-permute-start = (bf16[1,32,1024]{2,1,0:T(8,128)(2,1)}, bf16[1,32,1024]{2,1,0:T(8,128)(2,1)S(1)}, u32[]{:S(2)}, u32[]{:S(2)}) collective-permute-start(bf16[1,32,1024]{2,1,0:T(8,128)(2,1)} %refs_2_.1), channel_id=1, source_target_pairs={{0,0},{1,2},{2,1},{3,3},{4,4},{5,6},{6,5},{7,7},{8,8},{9,10},{10,9... | collective-permute-start | bytes 196616 | tf_op jit(solution)/shard_map/ppermute | solution.py:47
  2.1 7.5 %collective-permute-start.1 = (bf16[1,32,1024]{2,1,0:T(8,128)(2,1)}, bf16[1,32,1024]{2,1,0:T(8,128)(2,1)S(1)}, u32[]{:S(2)}, u32[]{:S(2)}) collective-permute-start(bf16[1,32,1024]{2,1,0:T(8,128)(2,1)} %refs_2_.1), channel_id=1, source_target_pairs={{0,4},{1,6},{2,5},{3,7},{4,8},{5,10},{6,9},{7,11},{8,12},{9,14},{1... | collective-permute-start | bytes 196616 | tf_op jit(solution)/shard_map/ppermute | solution.py:47
  5.2 7.0 %collective-permute-start.2 = (bf16[1,32,1024]{2,1,0:T(8,128)(2,1)}, bf16[1,32,1024]{2,1,0:T(8,128)(2,1)S(1)}, u32[]{:S(2)}, u32[]{:S(2)}) collective-permute-start(bf16[1,32,1024]{2,1,0:T(8,128)(2,1)} %refs_2_.1), channel_id=1, source_target_pairs={{0,8},{1,10},{2,9},{3,11},{4,12},{5,14},{6,13},{7,15},{8,0},{9,2},... | collective-permute-start | bytes 196616 | tf_op jit(solution)/shard_map/ppermute | solution.py:47
  7.8 5.1 %collective-permute-start.3 = (bf16[1,32,1024]{2,1,0:T(8,128)(2,1)}, bf16[1,32,1024]{2,1,0:T(8,128)(2,1)S(1)}, u32[]{:S(2)}, u32[]{:S(2)}) collective-permute-start(bf16[1,32,1024]{2,1,0:T(8,128)(2,1)} %refs_2_.1), channel_id=1, source_target_pairs={{0,12},{1,14},{2,13},{3,15},{4,0},{5,2},{6,1},{7,3},{8,4},{9,6},{1... | collective-permute-start | bytes 196616 | tf_op jit(solution)/shard_map/ppermute | solution.py:47
  9.1 3.7 %copy-start = (bf16[1,32,1024]{2,1,0:T(8,128)(2,1)}, bf16[1,32,1024]{2,1,0:T(8,128)(2,1)S(1)}, u32[]{:S(2)}) copy-start(bf16[1,32,1024]{2,1,0:T(8,128)(2,1)S(1)} %collective-permute-done.refs_6_) | copy-start | bytes 196612
  9.7 3.2 %copy-start.1 = (bf16[1,32,1024]{2,1,0:T(8,128)(2,1)}, bf16[1,32,1024]{2,1,0:T(8,128)(2,1)S(1)}, u32[]{:S(2)}) copy-start(bf16[1,32,1024]{2,1,0:T(8,128)(2,1)S(1)} %collective-permute-done.1.refs_7_) | copy-start | bytes 196612
  12.2 0.7 %copy-start.2 = (bf16[1,32,1024]{2,1,0:T(8,128)(2,1)}, bf16[1,32,1024]{2,1,0:T(8,128)(2,1)S(1)}, u32[]{:S(2)}) copy-start(bf16[1,32,1024]{2,1,0:T(8,128)(2,1)S(1)} %collective-permute-done.2.refs_8_) | copy-start | bytes 196612
  12.8 0.6 %copy-start.3 = (bf16[1,32,1024]{2,1,0:T(8,128)(2,1)}, bf16[1,32,1024]{2,1,0:T(8,128)(2,1)S(1)}, u32[]{:S(2)}) copy-start(bf16[1,32,1024]{2,1,0:T(8,128)(2,1)S(1)} %collective-permute-done.3.refs_9_) | copy-start | bytes 196612
  19.8 3.7 %collective-permute-start.4 = (f32[40,1024]{1,0:T(8,128)}, f32[40,1024]{1,0:T(8,128)S(1)}, u32[]{:S(2)}, u32[]{:S(2)}) collective-permute-start(f32[40,1024]{1,0:T(8,128)} %pairs.1), channel_id=1, source_target_pairs={{0,1},{1,0},{2,3},{3,2},{4,5},{5,4},{6,7},{7,6},{8,9},{9,8},{10,11... | collective-permute-start | bytes 491528 | tf_op jit(solution)/shard_map/ppermute | solution.py:292
  24.1 3.6 %collective-permute-start.5 = (f32[8,128]{1,0:T(8,128)S(1)}, f32[8,128]{1,0:T(8,128)S(1)}, u32[]{:S(2)}, u32[]{:S(2)}) collective-permute-start(f32[8,128]{1,0:T(8,128)S(1)} %slice_add_fusion.1), channel_id=1, source_target_pairs={{0,2},{2,0},{1,3},{3,1},{4,6},{6,4},{5,7},{7,5},{8,10},{10,8},{9,1... | collective-permute-start | bytes 12296 | tf_op jit(solution)/shard_map/ppermute | solution.py:31
  27.7 3.6 %collective-permute-start.6 = (f32[8,128]{1,0:T(8,128)S(1)}, f32[8,128]{1,0:T(8,128)S(1)}, u32[]{:S(2)}, u32[]{:S(2)}) collective-permute-start(f32[8,128]{1,0:T(8,128)S(1)} %add.17), channel_id=1, source_target_pairs={{0,4},{4,0},{8,12},{12,8},{1,5},{5,1},{9,13},{13,9},{2,6},{6,2},{1... | collective-permute-start | bytes 12296 | tf_op jit(solution)/shard_map/ppermute | solution.py:31
  31.4 4.5 %collective-permute-start.7 = (f32[8,128]{1,0:T(8,128)S(1)}, f32[8,128]{1,0:T(8,128)S(1)}, u32[]{:S(2)}, u32[]{:S(2)}) collective-permute-start(f32[8,128]{1,0:T(8,128)S(1)} %add.18), channel_id=1, source_target_pairs={{0,8},{4,12},{8,0},{12,4},{1,9},{5,13},{9,1},{13,5},{2,10},{6,14},... | collective-permute-start | bytes 12296 | tf_op jit(solution)/shard_map/ppermute | solution.py:31

commit v2 on v1

--- a/solution.py
+++ b/solution.py
@@ -36,16 +36,17 @@
 def turned_boxes(orbitals):
     axes = ("slab", "orb", "rep")
     slabs, side = lax.axis_size("slab"), lax.axis_size("orb")
-    boxes = []
-    for d in range(slabs):
-        moves = [
-            ((s * side + x) * side + r, ((s + d) % slabs * side + r) * side + x)
-            for s in range(slabs)
-            for x in range(side)
-            for r in range(side)
-        ]
-        boxes.append(lax.ppermute(orbitals, axes, moves))
-    return boxes
+    moves = [
+        ((s * side + x) * side + r, (s * side + r) * side + x)
+        for s in range(slabs)
+        for x in range(side)
+        for r in range(side)
+    ]
+    turned = lax.ppermute(orbitals, axes, moves)
+    boxes = {0: turned}
+    for d in sorted(range(1, slabs), key=lambda d: -min(d, slabs - d)):
+        boxes[d] = passed_along(turned, "slab", d)
+    return [boxes[d] for d in range(slabs)]
 
 
 def halves(table):
@@ -138,9 +139,13 @@
 
 
 def pair_kernel(*refs, slab_count, orb_count, rep_count, halo_depth, turned):
-    partners, corners, own, kernel, plane_tab, edge_tab = refs[:6]
-    pools = refs[6:-4]
-    out, moved_box, filters, chosen = refs[-4:]
+    partners, corners, own, kernel, plane_source, edge_source = refs[:6]
+    pools = refs[6:-7]
+    out, moved_box, filters, chosen, plane_tab, edge_tab, arrived = refs[-7:]
+    plane_copy = pltpu.make_async_copy(plane_source, plane_tab, arrived.at[0])
+    edge_copy = pltpu.make_async_copy(edge_source, edge_tab, arrived.at[1])
+    plane_copy.start()
+    edge_copy.start()
     own_count, box_edge, plane = own.shape
     slot_count = partners.shape[1]
     tile = plane // RADIX
@@ -155,6 +160,8 @@
     c_ids = lane_ids % box_edge
     total = jnp.zeros((1, 1), jnp.float32)
     filters[...] = ordered_filters(kernel[...])
+    plane_copy.wait()
+    edge_copy.wait()
     for o in range(own_count):
         centre = own[o].astype(jnp.float32)
         filled = jnp.int32(0)
@@ -269,6 +276,7 @@
     plane_tab, edge_tab = fourier_tables(box_edge)
     smem = pl.BlockSpec(memory_space=pltpu.SMEM)
     vmem = pl.BlockSpec(memory_space=pltpu.VMEM)
+    whole = pl.BlockSpec(memory_space=pl.ANY)
     sums = pl.pallas_call(
         functools.partial(
             pair_kernel,
@@ -278,13 +286,16 @@
             halo_depth=halo_depth,
             turned=turned,
         ),
-        in_specs=[smem, smem, vmem, vmem, vmem, vmem] + [vmem] * len(pools),
+        in_specs=[smem, smem, vmem, vmem, whole, whole] + [vmem] * len(pools),
         out_specs=vmem,
         out_shape=jax.ShapeDtypeStruct((own_count * box_edge + 8, plane), jnp.float32),
         scratch_shapes=[
             pltpu.VMEM((PB, box_edge, plane), jnp.float32),
             pltpu.VMEM((box_edge, (RADIX - 1) * plane // RADIX), jnp.float32),
             pltpu.SMEM((partners.shape[1] + 1,), jnp.int32),
+            pltpu.VMEM(plane_tab.shape, jnp.bfloat16),
+            pltpu.VMEM(edge_tab.shape, jnp.bfloat16),
+            pltpu.SemaphoreType.DMA((2,)),
         ],
         name="pairs",
     )(partners, corners.T, orbitals, kernel, plane_tab, edge_tab, *pools)

time: 38.4 us -> 39.8 us (1.036)
  starting transfers between devices: 13.1 us -> 17 us
  waiting for transfers between devices: 12.9 us -> 10 us
  Pallas kernels: 6.33 us -> 6.73 us
    ppermute x3, starting transfers between devices: 2.23 us -> 5.74 us  [swapped_sum(): lax.ppermute(value, axis, [(i, i ^ step) for i in range(size)])]
    ppermute x3, waiting for transfers between devices: 7.91 us -> 5.85 us  [swapped_sum(): lax.ppermute(value, axis, [(i, i ^ step) for i in range(size)])]
    ppermute x4, waiting for transfers between devices: 3.72 us -> 2.91 us  [the longest x3 2.91 us: passed_along(): lax.ppermute(array, axis, [(i, (i + by) % size) for i in range(size)])]
    pallas_call x1, Pallas kernels: 6.33 us -> 6.73 us  [body(): pl.pallas_call(functools.partial(pair_kernel, slab_count=slab_count, orb_...]
where the time goes in v2:
time: 39.8 us; the launch traced here: 39.5 us
  starting transfers between devices  17 us (43%)
  waiting for transfers between devices  10 us (25%)
  Pallas kernels  6.73 us (17%)
  between operations  2.43 us (6%)
  other arithmetic  2.27 us (6%)
  local copies, waits for them, and re-layouts  1.13 us (3%)
    ppermute x3, starting transfers between devices, passed_along(): lax.ppermute(array, axis, [(i, (i + by) % size) for i in range(size)])  6.99 us
    pallas_call x1, Pallas kernels, body(): pl.pallas_call(functools.partial(pair_kernel, slab_count=slab_count, orb_...  6.73 us
    ppermute x3, waiting for transfers between devices, swapped_sum(): lax.ppermute(value, axis, [(i, i ^ step) for i in range(size)])  5.85 us
    ppermute x3, starting transfers between devices, swapped_sum(): lax.ppermute(value, axis, [(i, i ^ step) for i in range(size)])  5.74 us
    ppermute x3, waiting for transfers between devices, passed_along(): lax.ppermute(array, axis, [(i, (i + by) % size) for i in range(size)])  2.91 us
    ppermute x1, starting transfers between devices, body(): other = lax.ppermute(sums, 'rep', [(i, i ^ 1) for i in range(rep_count)])  2.75 us
    reshape x1, other arithmetic, body(): exchange = (sums[:held] + other[:held]).reshape(own_count, box_edge, plane)  1.58 us
    ppermute x1, starting transfers between devices, turned_boxes(): turned = lax.ppermute(orbitals, axes, moves)  1.5 us
  transfers between devices with their start and end apart: 8, of which 7 were waited for; matrix products, arithmetic and copies ran while one was open for 4% of the time, Pallas kernels for 0%

profile of v2, /device:TPU:0, one launch (start us, length us, event | category | flops | bytes accessed | tf_op | source)
XLA Modules:
  0.0 39.5 jit_solution(8027200092559046207)
XLA Ops:
  0.6 1.5 %collective-permute-start = (bf16[1,32,1024]{2,1,0:T(8,128)(2,1)}, bf16[1,32,1024]{2,1,0:T(8,128)(2,1)S(1)}, u32[]{:S(2)}, u32[]{:S(2)}) collective-permute-start(bf16[1,32,1024]{2,1,0:T(8,128)(2,1)} %refs_2_.1), channel_id=1, source_target_pairs={{0,0},{1,2},{2,1},{3,3},{4,4},{5,6},{6,5},{7,7},{8,8},{9,10},{10,9... | collective-permute-start | bytes 196616 | tf_op jit(solution)/shard_map/ppermute | solution.py:45
  2.1 0.0 collective-permute-done.refs_6_
  2.1 0.0 copy-start
  2.1 3.1 %collective-permute-start.1 = (bf16[1,32,1024]{2,1,0:T(8,128)(2,1)S(1)}, bf16[1,32,1024]{2,1,0:T(8,128)(2,1)S(1)}, u32[]{:S(2)}, u32[]{:S(2)}) collective-permute-start(bf16[1,32,1024]{2,1,0:T(8,128)(2,1)S(1)} %collective-permute-done.refs_6_), channel_id=1, source_target_pairs={{0,4},{4,8},{8,12},{12,0},{1,5},{5,9},{9,13},{13,1},{2,6},{6,10},{... | collective-permute-start | bytes 196616 | tf_op jit(solution)/shard_map/ppermute | solution.py:20
  5.2 2.6 %collective-permute-start.2 = (bf16[1,32,1024]{2,1,0:T(8,128)(2,1)S(1)}, bf16[1,32,1024]{2,1,0:T(8,128)(2,1)S(1)}, u32[]{:S(2)}, u32[]{:S(2)}) collective-permute-start(bf16[1,32,1024]{2,1,0:T(8,128)(2,1)S(1)} %collective-permute-done.refs_6_), channel_id=1, source_target_pairs={{0,8},{4,12},{8,0},{12,4},{1,9},{5,13},{9,1},{13,5},{2,10},{6,14},... | collective-permute-start | bytes 196616 | tf_op jit(solution)/shard_map/ppermute | solution.py:20
  7.8 1.3 %collective-permute-start.3 = (bf16[1,32,1024]{2,1,0:T(8,128)(2,1)S(1)}, bf16[1,32,1024]{2,1,0:T(8,128)(2,1)S(1)}, u32[]{:S(2)}, u32[]{:S(2)}) collective-permute-start(bf16[1,32,1024]{2,1,0:T(8,128)(2,1)S(1)} %collective-permute-done.refs_6_), channel_id=1, source_target_pairs={{0,12},{4,0},{8,4},{12,8},{1,13},{5,1},{9,5},{13,9},{2,14},{6,2},{... | collective-permute-start | bytes 196616 | tf_op jit(solution)/shard_map/ppermute | solution.py:20
  9.1 0.3 collective-permute-done.1.refs_7_
  9.5 0.0 copy-start.1
  9.5 0.9 %collective-permute-done.2.refs_8_ = bf16[1,32,1024]{2,1,0:T(8,128)(2,1)S(1)} collective-permute-done((bf16[1,32,1024]{2,1,0:T(8,128)(2,1)S(1)}, bf16[1,32,1024]{2,1,0:T(8,128)(2,1)S(1)}, u32[]{:S(2)}, u32[]{:S(2)}) %collective-permute-start.2) | collective-permute-done | bytes 65568 | tf_op jit(solution)/shard_map/ppermute | solution.py:20
  10.4 0.0 copy-start.2
  10.4 1.7 %collective-permute-done.3.refs_9_ = bf16[1,32,1024]{2,1,0:T(8,128)(2,1)S(1)} collective-permute-done((bf16[1,32,1024]{2,1,0:T(8,128)(2,1)S(1)}, bf16[1,32,1024]{2,1,0:T(8,128)(2,1)S(1)}, u32[]{:S(2)}, u32[]{:S(2)}) %collective-permute-start.3) | collective-permute-done | bytes 65568 | tf_op jit(solution)/shard_map/ppermute | solution.py:20
  12.0 0.0 copy-start.3
  12.0 0.0 copy-done
  12.0 0.0 copy-done.1
  12.0 0.0 copy-done.2
  12.1 0.6 %copy-done.3 = bf16[1,32,1024]{2,1,0:T(8,128)(2,1)} copy-done((bf16[1,32,1024]{2,1,0:T(8,128)(2,1)}, bf16[1,32,1024]{2,1,0:T(8,128)(2,1)S(1)}, u32[]{:S(2)}) %copy-start.3) | copy-done | bytes 65560
  12.7 6.7 %pairs.1 = f32[40,1024]{1,0:T(8,128)} custom-call(s32[1,24]{1,0:T(1,128)} %refs_0_.1, s32[3,8]{1,0:T(4,128)} %bitcast.4, bf16[1,32,1024]{2,1,0:T(8,128)(2,1)} %refs_2_.1, f32[32,1024]{1,0:T(8,128)} %refs_3_.1, bf16[2,3,256,512]{3,2,1,0:T(8,128)(2,1)} %constant.8.clone.refs_4_, bf16[2,2,256,256]{3,2,1,0:T(8,128)(2,1)} %constant.9.clone.refs_5_, ...), custom_call_target="tpu_custom_call" | custom-call | tf_op jit(solution)/shard_map/pairs/pallas_call | solution.py:280
  19.4 2.7 %collective-permute-start.4 = (f32[40,1024]{1,0:T(8,128)}, f32[40,1024]{1,0:T(8,128)S(1)}, u32[]{:S(2)}, u32[]{:S(2)}) collective-permute-start(f32[40,1024]{1,0:T(8,128)} %pairs.1), channel_id=1, source_target_pairs={{0,1},{1,0},{2,3},{3,2},{4,5},{5,4},{6,7},{7,6},{8,9},{9,8},{10,11... | collective-permute-start | bytes 491528 | tf_op jit(solution)/shard_map/ppermute | solution.py:303
  22.1 1.2 %collective-permute-done.4 = f32[40,1024]{1,0:T(8,128)S(1)} collective-permute-done((f32[40,1024]{1,0:T(8,128)}, f32[40,1024]{1,0:T(8,128)S(1)}, u32[]{:S(2)}, u32[]{:S(2)}) %collective-permute-start.4) | collective-permute-done | bytes 163872 | tf_op jit(solution)/shard_map/ppermute | solution.py:303
  23.4 0.7 %slice_add_fusion.1 = f32[8,128]{1,0:T(8,128)S(1)} fusion(f32[40,1024]{1,0:T(8,128)S(1)} %collective-permute-done.4, f32[40,1024]{1,0:T(8,128)} %pairs.1), kind=kLoop, calls=%fused_computation.2 | loop fusion | flops 1024 | bytes 12288 | tf_op jit(solution)/shard_map/add | solution.py:304
  24.1 3.5 %collective-permute-start.5 = (f32[8,128]{1,0:T(8,128)S(1)}, f32[8,128]{1,0:T(8,128)S(1)}, u32[]{:S(2)}, u32[]{:S(2)}) collective-permute-start(f32[8,128]{1,0:T(8,128)S(1)} %slice_add_fusion.1), channel_id=1, source_target_pairs={{0,2},{2,0},{1,3},{3,1},{4,6},{6,4},{5,7},{7,5},{8,10},{10,8},{9,1... | collective-permute-start | bytes 12296 | tf_op jit(solution)/shard_map/ppermute | solution.py:31
  27.5 1.6 %collective-permute-done.5 = f32[8,128]{1,0:T(8,128)S(1)} collective-permute-done((f32[8,128]{1,0:T(8,128)S(1)}, f32[8,128]{1,0:T(8,128)S(1)}, u32[]{:S(2)}, u32[]{:S(2)}) %collective-permute-start.5) | collective-permute-done | bytes 4128 | tf_op jit(solution)/shard_map/ppermute | solution.py:31
  29.1 0.6 %collective-permute-start.6 = (f32[8,128]{1,0:T(8,128)S(1)}, f32[8,128]{1,0:T(8,128)S(1)}, u32[]{:S(2)}, u32[]{:S(2)}) collective-permute-start(f32[8,128]{1,0:T(8,128)S(1)} %add.17), channel_id=1, source_target_pairs={{0,4},{4,0},{8,12},{12,8},{1,5},{5,1},{9,13},{13,9},{2,6},{6,2},{1... | collective-permute-start | bytes 12296 | tf_op jit(solution)/shard_map/ppermute | solution.py:31
  29.7 3.0 %collective-permute-done.6 = f32[8,128]{1,0:T(8,128)S(1)} collective-permute-done((f32[8,128]{1,0:T(8,128)S(1)}, f32[8,128]{1,0:T(8,128)S(1)}, u32[]{:S(2)}, u32[]{:S(2)}) %collective-permute-start.6) | collective-permute-done | bytes 4128 | tf_op jit(solution)/shard_map/ppermute | solution.py:31
  32.7 1.7 %collective-permute-start.7 = (f32[8,128]{1,0:T(8,128)S(1)}, f32[8,128]{1,0:T(8,128)S(1)}, u32[]{:S(2)}, u32[]{:S(2)}) collective-permute-start(f32[8,128]{1,0:T(8,128)S(1)} %add.18), channel_id=1, source_target_pairs={{0,8},{4,12},{8,0},{12,4},{1,9},{5,13},{9,1},{13,5},{2,10},{6,14},... | collective-permute-start | bytes 12296 | tf_op jit(solution)/shard_map/ppermute | solution.py:31
  34.4 1.6 %fusion = f32[1,32,1024]{2,1,0:T(8,128)} fusion(f32[40,1024]{1,0:T(8,128)S(1)} %collective-permute-done.4, f32[40,1024]{1,0:T(8,128)} %pairs.1), kind=kLoop, calls=%fused_computation.1 | loop fusion | flops 32768 | bytes 393216 | tf_op jit(solution)/shard_map/reshape | solution.py:305
  36.0 1.2 %collective-permute-done.7 = f32[8,128]{1,0:T(8,128)S(1)} collective-permute-done((f32[8,128]{1,0:T(8,128)S(1)}, f32[8,128]{1,0:T(8,128)S(1)}, u32[]{:S(2)}, u32[]{:S(2)}) %collective-permute-start.7) | collective-permute-done | bytes 4128 | tf_op jit(solution)/shard_map/ppermute | solution.py:31
  37.3 0.5 %slice.19 = f32[1,1]{1,0:T(1,128)} slice(f32[8,128]{1,0:T(8,128)S(1)} %add.19), slice={[0:1], [0:1]} | slice | bytes 8 | tf_op jit(solution)/shard_map/slice | solution.py:306
  (3 shorter events, 0.0 us)
Async XLA Ops:
  0.6 1.5 %collective-permute-start = (bf16[1,32,1024]{2,1,0:T(8,128)(2,1)}, bf16[1,32,1024]{2,1,0:T(8,128)(2,1)S(1)}, u32[]{:S(2)}, u32[]{:S(2)}) collective-permute-start(bf16[1,32,1024]{2,1,0:T(8,128)(2,1)} %refs_2_.1), channel_id=1, source_target_pairs={{0,0},{1,2},{2,1},{3,3},{4,4},{5,6},{6,5},{7,7},{8,8},{9,10},{10,9... | collective-permute-start | bytes 196616 | tf_op jit(solution)/shard_map/ppermute | solution.py:45
  2.1 9.9 %copy-start = (bf16[1,32,1024]{2,1,0:T(8,128)(2,1)}, bf16[1,32,1024]{2,1,0:T(8,128)(2,1)S(1)}, u32[]{:S(2)}) copy-start(bf16[1,32,1024]{2,1,0:T(8,128)(2,1)S(1)} %collective-permute-done.refs_6_) | copy-start | bytes 196612
  2.1 7.3 %collective-permute-start.1 = (bf16[1,32,1024]{2,1,0:T(8,128)(2,1)S(1)}, bf16[1,32,1024]{2,1,0:T(8,128)(2,1)S(1)}, u32[]{:S(2)}, u32[]{:S(2)}) collective-permute-start(bf16[1,32,1024]{2,1,0:T(8,128)(2,1)S(1)} %collective-permute-done.refs_6_), channel_id=1, source_target_pairs={{0,4},{4,8},{8,12},{12,0},{1,5},{5,9},{9,13},{13,1},{2,6},{6,10},{... | collective-permute-start | bytes 196616 | tf_op jit(solution)/shard_map/ppermute | solution.py:20
  5.2 5.2 %collective-permute-start.2 = (bf16[1,32,1024]{2,1,0:T(8,128)(2,1)S(1)}, bf16[1,32,1024]{2,1,0:T(8,128)(2,1)S(1)}, u32[]{:S(2)}, u32[]{:S(2)}) collective-permute-start(bf16[1,32,1024]{2,1,0:T(8,128)(2,1)S(1)} %collective-permute-done.refs_6_), channel_id=1, source_target_pairs={{0,8},{4,12},{8,0},{12,4},{1,9},{5,13},{9,1},{13,5},{2,10},{6,14},... | collective-permute-start | bytes 196616 | tf_op jit(solution)/shard_map/ppermute | solution.py:20
  7.8 4.3 %collective-permute-start.3 = (bf16[1,32,1024]{2,1,0:T(8,128)(2,1)S(1)}, bf16[1,32,1024]{2,1,0:T(8,128)(2,1)S(1)}, u32[]{:S(2)}, u32[]{:S(2)}) collective-permute-start(bf16[1,32,1024]{2,1,0:T(8,128)(2,1)S(1)} %collective-permute-done.refs_6_), channel_id=1, source_target_pairs={{0,12},{4,0},{8,4},{12,8},{1,13},{5,1},{9,5},{13,9},{2,14},{6,2},{... | collective-permute-start | bytes 196616 | tf_op jit(solution)/shard_map/ppermute | solution.py:20
  9.5 2.6 %copy-start.1 = (bf16[1,32,1024]{2,1,0:T(8,128)(2,1)}, bf16[1,32,1024]{2,1,0:T(8,128)(2,1)S(1)}, u32[]{:S(2)}) copy-start(bf16[1,32,1024]{2,1,0:T(8,128)(2,1)S(1)} %collective-permute-done.1.refs_7_) | copy-start | bytes 196612
  10.4 1.7 %copy-start.2 = (bf16[1,32,1024]{2,1,0:T(8,128)(2,1)}, bf16[1,32,1024]{2,1,0:T(8,128)(2,1)S(1)}, u32[]{:S(2)}) copy-start(bf16[1,32,1024]{2,1,0:T(8,128)(2,1)S(1)} %collective-permute-done.2.refs_8_) | copy-start | bytes 196612
  12.0 0.6 %copy-start.3 = (bf16[1,32,1024]{2,1,0:T(8,128)(2,1)}, bf16[1,32,1024]{2,1,0:T(8,128)(2,1)S(1)}, u32[]{:S(2)}) copy-start(bf16[1,32,1024]{2,1,0:T(8,128)(2,1)S(1)} %collective-permute-done.3.refs_9_) | copy-start | bytes 196612
  19.4 4.0 %collective-permute-start.4 = (f32[40,1024]{1,0:T(8,128)}, f32[40,1024]{1,0:T(8,128)S(1)}, u32[]{:S(2)}, u32[]{:S(2)}) collective-permute-start(f32[40,1024]{1,0:T(8,128)} %pairs.1), channel_id=1, source_target_pairs={{0,1},{1,0},{2,3},{3,2},{4,5},{5,4},{6,7},{7,6},{8,9},{9,8},{10,11... | collective-permute-start | bytes 491528 | tf_op jit(solution)/shard_map/ppermute | solution.py:303
  24.1 5.1 %collective-permute-start.5 = (f32[8,128]{1,0:T(8,128)S(1)}, f32[8,128]{1,0:T(8,128)S(1)}, u32[]{:S(2)}, u32[]{:S(2)}) collective-permute-start(f32[8,128]{1,0:T(8,128)S(1)} %slice_add_fusion.1), channel_id=1, source_target_pairs={{0,2},{2,0},{1,3},{3,1},{4,6},{6,4},{5,7},{7,5},{8,10},{10,8},{9,1... | collective-permute-start | bytes 12296 | tf_op jit(solution)/shard_map/ppermute | solution.py:31
  29.1 3.6 %collective-permute-start.6 = (f32[8,128]{1,0:T(8,128)S(1)}, f32[8,128]{1,0:T(8,128)S(1)}, u32[]{:S(2)}, u32[]{:S(2)}) collective-permute-start(f32[8,128]{1,0:T(8,128)S(1)} %add.17), channel_id=1, source_target_pairs={{0,4},{4,0},{8,12},{12,8},{1,5},{5,1},{9,13},{13,9},{2,6},{6,2},{1... | collective-permute-start | bytes 12296 | tf_op jit(solution)/shard_map/ppermute | solution.py:31
  32.7 4.5 %collective-permute-start.7 = (f32[8,128]{1,0:T(8,128)S(1)}, f32[8,128]{1,0:T(8,128)S(1)}, u32[]{:S(2)}, u32[]{:S(2)}) collective-permute-start(f32[8,128]{1,0:T(8,128)S(1)} %add.18), channel_id=1, source_target_pairs={{0,8},{4,12},{8,0},{12,4},{1,9},{5,13},{9,1},{13,5},{2,10},{6,14},... | collective-permute-start | bytes 12296 | tf_op jit(solution)/shard_map/ppermute | solution.py:31

commit v3 on v1

--- a/solution.py
+++ b/solution.py
@@ -36,16 +36,16 @@
 def turned_boxes(orbitals):
     axes = ("slab", "orb", "rep")
     slabs, side = lax.axis_size("slab"), lax.axis_size("orb")
-    boxes = []
-    for d in range(slabs):
+    boxes = {}
+    for d in sorted(range(slabs), key=lambda d: -min(d, slabs - d)):
         moves = [
             ((s * side + x) * side + r, ((s + d) % slabs * side + r) * side + x)
             for s in range(slabs)
             for x in range(side)
             for r in range(side)
         ]
-        boxes.append(lax.ppermute(orbitals, axes, moves))
-    return boxes
+        boxes[d] = lax.ppermute(orbitals, axes, moves)
+    return [boxes[d] for d in range(slabs)]
 
 
 def halves(table):

time: 38.4 us -> 38.4 us (level)
  no operation moved by 1% of the time
where the time goes in v3:
time: 38.4 us; the launch traced here: 38.2 us
  starting transfers between devices  13.4 us (35%)
  waiting for transfers between devices  12.7 us (33%)
  Pallas kernels  6.33 us (16%)
  between operations  2.43 us (6%)
  other arithmetic  2.27 us (6%)
  local copies, waits for them, and re-layouts  1.13 us (3%)
    ppermute x4, starting transfers between devices, turned_boxes(): boxes[d] = lax.ppermute(orbitals, axes, moves)  8.49 us
    ppermute x3, waiting for transfers between devices, swapped_sum(): lax.ppermute(value, axis, [(i, i ^ step) for i in range(size)])  7.69 us
    pallas_call x1, Pallas kernels, body(): pl.pallas_call(functools.partial(pair_kernel, slab_count=slab_count, orb_...  6.33 us
    ppermute x4, waiting for transfers between devices, turned_boxes(): boxes[d] = lax.ppermute(orbitals, axes, moves)  3.72 us
    ppermute x3, starting transfers between devices, swapped_sum(): lax.ppermute(value, axis, [(i, i ^ step) for i in range(size)])  2.45 us
    ppermute x1, starting transfers between devices, body(): other = lax.ppermute(sums, 'rep', [(i, i ^ 1) for i in range(rep_count)])  2.42 us
    reshape x1, other arithmetic, body(): exchange = (sums[:held] + other[:held]).reshape(own_count, box_edge, plane)  1.58 us
    ppermute x1, waiting for transfers between devices, body(): other = lax.ppermute(sums, 'rep', [(i, i ^ 1) for i in range(rep_count)])  1.24 us
  transfers between devices with their start and end apart: 8, of which 7 were waited for; matrix products, arithmetic and copies ran while one was open for 4% of the time, Pallas kernels for 0%

profile of v3, /device:TPU:0, one launch (start us, length us, event | category | flops | bytes accessed | tf_op | source)
XLA Modules:
  0.0 38.2 jit_solution(209503954135759200)
XLA Ops:
  0.6 1.5 %collective-permute-start = (bf16[1,32,1024]{2,1,0:T(8,128)(2,1)}, bf16[1,32,1024]{2,1,0:T(8,128)(2,1)S(1)}, u32[]{:S(2)}, u32[]{:S(2)}) collective-permute-start(bf16[1,32,1024]{2,1,0:T(8,128)(2,1)} %refs_2_.1), channel_id=1, source_target_pairs={{0,0},{1,2},{2,1},{3,3},{4,4},{5,6},{6,5},{7,7},{8,8},{9,10},{10,9... | collective-permute-start | bytes 196616 | tf_op jit(solution)/shard_map/ppermute | solution.py:47
  2.1 3.1 %collective-permute-start.1 = (bf16[1,32,1024]{2,1,0:T(8,128)(2,1)}, bf16[1,32,1024]{2,1,0:T(8,128)(2,1)S(1)}, u32[]{:S(2)}, u32[]{:S(2)}) collective-permute-start(bf16[1,32,1024]{2,1,0:T(8,128)(2,1)} %refs_2_.1), channel_id=1, source_target_pairs={{0,4},{1,6},{2,5},{3,7},{4,8},{5,10},{6,9},{7,11},{8,12},{9,14},{1... | collective-permute-start | bytes 196616 | tf_op jit(solution)/shard_map/ppermute | solution.py:47
  5.2 2.6 %collective-permute-start.2 = (bf16[1,32,1024]{2,1,0:T(8,128)(2,1)}, bf16[1,32,1024]{2,1,0:T(8,128)(2,1)S(1)}, u32[]{:S(2)}, u32[]{:S(2)}) collective-permute-start(bf16[1,32,1024]{2,1,0:T(8,128)(2,1)} %refs_2_.1), channel_id=1, source_target_pairs={{0,8},{1,10},{2,9},{3,11},{4,12},{5,14},{6,13},{7,15},{8,0},{9,2},... | collective-permute-start | bytes 196616 | tf_op jit(solution)/shard_map/ppermute | solution.py:47
  7.8 1.3 %collective-permute-start.3 = (bf16[1,32,1024]{2,1,0:T(8,128)(2,1)}, bf16[1,32,1024]{2,1,0:T(8,128)(2,1)S(1)}, u32[]{:S(2)}, u32[]{:S(2)}) collective-permute-start(bf16[1,32,1024]{2,1,0:T(8,128)(2,1)} %refs_2_.1), channel_id=1, source_target_pairs={{0,12},{1,14},{2,13},{3,15},{4,0},{5,2},{6,1},{7,3},{8,4},{9,6},{1... | collective-permute-start | bytes 196616 | tf_op jit(solution)/shard_map/ppermute | solution.py:47
  9.1 0.0 collective-permute-done.refs_6_
  9.1 0.0 copy-start
  9.1 0.5 %collective-permute-done.1.refs_7_ = bf16[1,32,1024]{2,1,0:T(8,128)(2,1)S(1)} collective-permute-done((bf16[1,32,1024]{2,1,0:T(8,128)(2,1)}, bf16[1,32,1024]{2,1,0:T(8,128)(2,1)S(1)}, u32[]{:S(2)}, u32[]{:S(2)}) %collective-permute-start.1) | collective-permute-done | bytes 65568 | tf_op jit(solution)/shard_map/ppermute | solution.py:47
  9.7 0.0 copy-start.1
  9.7 2.5 %collective-permute-done.2.refs_8_ = bf16[1,32,1024]{2,1,0:T(8,128)(2,1)S(1)} collective-permute-done((bf16[1,32,1024]{2,1,0:T(8,128)(2,1)}, bf16[1,32,1024]{2,1,0:T(8,128)(2,1)S(1)}, u32[]{:S(2)}, u32[]{:S(2)}) %collective-permute-start.2) | collective-permute-done | bytes 65568 | tf_op jit(solution)/shard_map/ppermute | solution.py:47
  12.2 0.0 copy-start.2
  12.2 0.7 %collective-permute-done.3.refs_9_ = bf16[1,32,1024]{2,1,0:T(8,128)(2,1)S(1)} collective-permute-done((bf16[1,32,1024]{2,1,0:T(8,128)(2,1)}, bf16[1,32,1024]{2,1,0:T(8,128)(2,1)S(1)}, u32[]{:S(2)}, u32[]{:S(2)}) %collective-permute-start.3) | collective-permute-done | bytes 65568 | tf_op jit(solution)/shard_map/ppermute | solution.py:47
  12.8 0.0 copy-start.3
  12.9 0.0 copy-done
  12.9 0.0 copy-done.1
  12.9 0.0 copy-done.2
  12.9 0.6 %copy-done.3 = bf16[1,32,1024]{2,1,0:T(8,128)(2,1)} copy-done((bf16[1,32,1024]{2,1,0:T(8,128)(2,1)}, bf16[1,32,1024]{2,1,0:T(8,128)(2,1)S(1)}, u32[]{:S(2)}) %copy-start.3) | copy-done | bytes 65560
  13.5 6.3 %pairs.1 = f32[40,1024]{1,0:T(8,128)} custom-call(s32[1,24]{1,0:T(1,128)} %refs_0_.1, s32[3,8]{1,0:T(4,128)} %bitcast.4, bf16[1,32,1024]{2,1,0:T(8,128)(2,1)} %refs_2_.1, f32[32,1024]{1,0:T(8,128)} %refs_3_.1, bf16[2,3,256,512]{3,2,1,0:T(8,128)(2,1)} %constant.8.clone.refs_4_, bf16[2,2,256,256]{3,2,1,0:T(8,128)(2,1)} %constant.9.clone.refs_5_, ...), custom_call_target="tpu_custom_call" | custom-call | tf_op jit(solution)/shard_map/pairs/pallas_call | solution.py:272
  19.8 2.4 %collective-permute-start.4 = (f32[40,1024]{1,0:T(8,128)}, f32[40,1024]{1,0:T(8,128)S(1)}, u32[]{:S(2)}, u32[]{:S(2)}) collective-permute-start(f32[40,1024]{1,0:T(8,128)} %pairs.1), channel_id=1, source_target_pairs={{0,1},{1,0},{2,3},{3,2},{4,5},{5,4},{6,7},{7,6},{8,9},{9,8},{10,11... | collective-permute-start | bytes 491528 | tf_op jit(solution)/shard_map/ppermute | solution.py:292
  22.2 1.2 %collective-permute-done.4 = f32[40,1024]{1,0:T(8,128)S(1)} collective-permute-done((f32[40,1024]{1,0:T(8,128)}, f32[40,1024]{1,0:T(8,128)S(1)}, u32[]{:S(2)}, u32[]{:S(2)}) %collective-permute-start.4) | collective-permute-done | bytes 163872 | tf_op jit(solution)/shard_map/ppermute | solution.py:292
  23.5 0.7 %slice_add_fusion.1 = f32[8,128]{1,0:T(8,128)S(1)} fusion(f32[40,1024]{1,0:T(8,128)S(1)} %collective-permute-done.4, f32[40,1024]{1,0:T(8,128)} %pairs.1), kind=kLoop, calls=%fused_computation.2 | loop fusion | flops 1024 | bytes 12288 | tf_op jit(solution)/shard_map/add | solution.py:293
  24.1 0.5 %collective-permute-start.5 = (f32[8,128]{1,0:T(8,128)S(1)}, f32[8,128]{1,0:T(8,128)S(1)}, u32[]{:S(2)}, u32[]{:S(2)}) collective-permute-start(f32[8,128]{1,0:T(8,128)S(1)} %slice_add_fusion.1), channel_id=1, source_target_pairs={{0,2},{2,0},{1,3},{3,1},{4,6},{6,4},{5,7},{7,5},{8,10},{10,8},{9,1... | collective-permute-start | bytes 12296 | tf_op jit(solution)/shard_map/ppermute | solution.py:31
  24.7 3.1 %collective-permute-done.5 = f32[8,128]{1,0:T(8,128)S(1)} collective-permute-done((f32[8,128]{1,0:T(8,128)S(1)}, f32[8,128]{1,0:T(8,128)S(1)}, u32[]{:S(2)}, u32[]{:S(2)}) %collective-permute-start.5) | collective-permute-done | bytes 4128 | tf_op jit(solution)/shard_map/ppermute | solution.py:31
  27.7 0.2 collective-permute-start.6
  28.0 3.4 %collective-permute-done.6 = f32[8,128]{1,0:T(8,128)S(1)} collective-permute-done((f32[8,128]{1,0:T(8,128)S(1)}, f32[8,128]{1,0:T(8,128)S(1)}, u32[]{:S(2)}, u32[]{:S(2)}) %collective-permute-start.6) | collective-permute-done | bytes 4128 | tf_op jit(solution)/shard_map/ppermute | solution.py:31
  31.4 1.7 %collective-permute-start.7 = (f32[8,128]{1,0:T(8,128)S(1)}, f32[8,128]{1,0:T(8,128)S(1)}, u32[]{:S(2)}, u32[]{:S(2)}) collective-permute-start(f32[8,128]{1,0:T(8,128)S(1)} %add.18), channel_id=1, source_target_pairs={{0,8},{4,12},{8,0},{12,4},{1,9},{5,13},{9,1},{13,5},{2,10},{6,14},... | collective-permute-start | bytes 12296 | tf_op jit(solution)/shard_map/ppermute | solution.py:31
  33.0 1.6 %fusion = f32[1,32,1024]{2,1,0:T(8,128)} fusion(f32[40,1024]{1,0:T(8,128)S(1)} %collective-permute-done.4, f32[40,1024]{1,0:T(8,128)} %pairs.1), kind=kLoop, calls=%fused_computation.1 | loop fusion | flops 32768 | bytes 393216 | tf_op jit(solution)/shard_map/reshape | solution.py:294
  34.6 1.2 %collective-permute-done.7 = f32[8,128]{1,0:T(8,128)S(1)} collective-permute-done((f32[8,128]{1,0:T(8,128)S(1)}, f32[8,128]{1,0:T(8,128)S(1)}, u32[]{:S(2)}, u32[]{:S(2)}) %collective-permute-start.7) | collective-permute-done | bytes 4128 | tf_op jit(solution)/shard_map/ppermute | solution.py:31
  35.9 0.5 %slice.19 = f32[1,1]{1,0:T(1,128)} slice(f32[8,128]{1,0:T(8,128)S(1)} %add.19), slice={[0:1], [0:1]} | slice | bytes 8 | tf_op jit(solution)/shard_map/slice | solution.py:295
  (3 shorter events, 0.0 us)
Async XLA Ops:
  0.6 8.5 %collective-permute-start = (bf16[1,32,1024]{2,1,0:T(8,128)(2,1)}, bf16[1,32,1024]{2,1,0:T(8,128)(2,1)S(1)}, u32[]{:S(2)}, u32[]{:S(2)}) collective-permute-start(bf16[1,32,1024]{2,1,0:T(8,128)(2,1)} %refs_2_.1), channel_id=1, source_target_pairs={{0,0},{1,2},{2,1},{3,3},{4,4},{5,6},{6,5},{7,7},{8,8},{9,10},{10,9... | collective-permute-start | bytes 196616 | tf_op jit(solution)/shard_map/ppermute | solution.py:47
  2.1 7.5 %collective-permute-start.1 = (bf16[1,32,1024]{2,1,0:T(8,128)(2,1)}, bf16[1,32,1024]{2,1,0:T(8,128)(2,1)S(1)}, u32[]{:S(2)}, u32[]{:S(2)}) collective-permute-start(bf16[1,32,1024]{2,1,0:T(8,128)(2,1)} %refs_2_.1), channel_id=1, source_target_pairs={{0,4},{1,6},{2,5},{3,7},{4,8},{5,10},{6,9},{7,11},{8,12},{9,14},{1... | collective-permute-start | bytes 196616 | tf_op jit(solution)/shard_map/ppermute | solution.py:47
  5.2 7.0 %collective-permute-start.2 = (bf16[1,32,1024]{2,1,0:T(8,128)(2,1)}, bf16[1,32,1024]{2,1,0:T(8,128)(2,1)S(1)}, u32[]{:S(2)}, u32[]{:S(2)}) collective-permute-start(bf16[1,32,1024]{2,1,0:T(8,128)(2,1)} %refs_2_.1), channel_id=1, source_target_pairs={{0,8},{1,10},{2,9},{3,11},{4,12},{5,14},{6,13},{7,15},{8,0},{9,2},... | collective-permute-start | bytes 196616 | tf_op jit(solution)/shard_map/ppermute | solution.py:47
  7.8 5.1 %collective-permute-start.3 = (bf16[1,32,1024]{2,1,0:T(8,128)(2,1)}, bf16[1,32,1024]{2,1,0:T(8,128)(2,1)S(1)}, u32[]{:S(2)}, u32[]{:S(2)}) collective-permute-start(bf16[1,32,1024]{2,1,0:T(8,128)(2,1)} %refs_2_.1), channel_id=1, source_target_pairs={{0,12},{1,14},{2,13},{3,15},{4,0},{5,2},{6,1},{7,3},{8,4},{9,6},{1... | collective-permute-start | bytes 196616 | tf_op jit(solution)/shard_map/ppermute | solution.py:47
  9.1 3.7 %copy-start = (bf16[1,32,1024]{2,1,0:T(8,128)(2,1)}, bf16[1,32,1024]{2,1,0:T(8,128)(2,1)S(1)}, u32[]{:S(2)}) copy-start(bf16[1,32,1024]{2,1,0:T(8,128)(2,1)S(1)} %collective-permute-done.refs_6_) | copy-start | bytes 196612
  9.7 3.2 %copy-start.1 = (bf16[1,32,1024]{2,1,0:T(8,128)(2,1)}, bf16[1,32,1024]{2,1,0:T(8,128)(2,1)S(1)}, u32[]{:S(2)}) copy-start(bf16[1,32,1024]{2,1,0:T(8,128)(2,1)S(1)} %collective-permute-done.1.refs_7_) | copy-start | bytes 196612
  12.2 0.7 %copy-start.2 = (bf16[1,32,1024]{2,1,0:T(8,128)(2,1)}, bf16[1,32,1024]{2,1,0:T(8,128)(2,1)S(1)}, u32[]{:S(2)}) copy-start(bf16[1,32,1024]{2,1,0:T(8,128)(2,1)S(1)} %collective-permute-done.2.refs_8_) | copy-start | bytes 196612
  12.8 0.6 %copy-start.3 = (bf16[1,32,1024]{2,1,0:T(8,128)(2,1)}, bf16[1,32,1024]{2,1,0:T(8,128)(2,1)S(1)}, u32[]{:S(2)}) copy-start(bf16[1,32,1024]{2,1,0:T(8,128)(2,1)S(1)} %collective-permute-done.3.refs_9_) | copy-start | bytes 196612
  19.8 3.7 %collective-permute-start.4 = (f32[40,1024]{1,0:T(8,128)}, f32[40,1024]{1,0:T(8,128)S(1)}, u32[]{:S(2)}, u32[]{:S(2)}) collective-permute-start(f32[40,1024]{1,0:T(8,128)} %pairs.1), channel_id=1, source_target_pairs={{0,1},{1,0},{2,3},{3,2},{4,5},{5,4},{6,7},{7,6},{8,9},{9,8},{10,11... | collective-permute-start | bytes 491528 | tf_op jit(solution)/shard_map/ppermute | solution.py:292
  24.1 3.6 %collective-permute-start.5 = (f32[8,128]{1,0:T(8,128)S(1)}, f32[8,128]{1,0:T(8,128)S(1)}, u32[]{:S(2)}, u32[]{:S(2)}) collective-permute-start(f32[8,128]{1,0:T(8,128)S(1)} %slice_add_fusion.1), channel_id=1, source_target_pairs={{0,2},{2,0},{1,3},{3,1},{4,6},{6,4},{5,7},{7,5},{8,10},{10,8},{9,1... | collective-permute-start | bytes 12296 | tf_op jit(solution)/shard_map/ppermute | solution.py:31
  27.7 3.6 %collective-permute-start.6 = (f32[8,128]{1,0:T(8,128)S(1)}, f32[8,128]{1,0:T(8,128)S(1)}, u32[]{:S(2)}, u32[]{:S(2)}) collective-permute-start(f32[8,128]{1,0:T(8,128)S(1)} %add.17), channel_id=1, source_target_pairs={{0,4},{4,0},{8,12},{12,8},{1,5},{5,1},{9,13},{13,9},{2,6},{6,2},{1... | collective-permute-start | bytes 12296 | tf_op jit(solution)/shard_map/ppermute | solution.py:31
  31.4 4.5 %collective-permute-start.7 = (f32[8,128]{1,0:T(8,128)S(1)}, f32[8,128]{1,0:T(8,128)S(1)}, u32[]{:S(2)}, u32[]{:S(2)}) collective-permute-start(f32[8,128]{1,0:T(8,128)S(1)} %add.18), channel_id=1, source_target_pairs={{0,8},{4,12},{8,0},{12,4},{1,9},{5,13},{9,1},{13,5},{2,10},{6,14},... | collective-permute-start | bytes 12296 | tf_op jit(solution)/shard_map/ppermute | solution.py:31

commit v4 on v1

--- a/solution.py
+++ b/solution.py
@@ -25,6 +25,12 @@
         size = lax.axis_size(axis)
         if size & (size - 1):
             value = lax.psum(value, axis)
+            continue
+        if size == 4:
+            first, second, third = (
+                lax.ppermute(value, axis, [(i, i ^ d) for i in range(size)]) for d in (1, 2, 3)
+            )
+            value = (value + first) + (second + third)
             continue
         step = 1
         while step < size:

time: 38.4 us -> 39.5 us (1.029)
  starting transfers between devices: 13.1 us -> 15.8 us
  waiting for transfers between devices: 12.9 us -> 11.2 us
    ppermute x3 -> x1, waiting for transfers between devices: 7.91 us -> 3.05 us  [swapped_sum(): lax.ppermute(value, axis, [(i, i ^ step) for i in range(size)])]
    ppermute x0 -> x3, starting transfers between devices: none -> 4.39 us  [swapped_sum(): lax.ppermute(value, axis, [(i, i ^ d) for i in range(size)])]
    ppermute x0 -> x3, waiting for transfers between devices: none -> 3.15 us  [swapped_sum(): lax.ppermute(value, axis, [(i, i ^ d) for i in range(size)])]
    ppermute x3 -> x1, starting transfers between devices: 2.23 us -> 0.55 us  [swapped_sum(): lax.ppermute(value, axis, [(i, i ^ step) for i in range(size)])]
  transfers between devices with their start and end apart: 8 -> 9, of which waited for: 7 -> 6; matrix products, arithmetic and copies ran while one was open for 4% -> 4% of each run, Pallas kernels for 0% -> 0%
where the time goes in v4:
time: 39.5 us; the launch traced here: 39.2 us
  starting transfers between devices  15.8 us (40%)
  waiting for transfers between devices  11.2 us (28%)
  Pallas kernels  6.34 us (16%)
  between operations  2.43 us (6%)
  other arithmetic  2.27 us (6%)
  local copies, waits for them, and re-layouts  1.14 us (3%)
    ppermute x4, starting transfers between devices, turned_boxes(): boxes.append(lax.ppermute(orbitals, axes, moves))  8.49 us
    pallas_call x1, Pallas kernels, body(): pl.pallas_call(functools.partial(pair_kernel, slab_count=slab_count, orb_...  6.34 us
    ppermute x3, starting transfers between devices, swapped_sum(): lax.ppermute(value, axis, [(i, i ^ d) for i in range(size)])  4.39 us
    ppermute x4, waiting for transfers between devices, turned_boxes(): boxes.append(lax.ppermute(orbitals, axes, moves))  3.72 us
    ppermute x3, waiting for transfers between devices, swapped_sum(): lax.ppermute(value, axis, [(i, i ^ d) for i in range(size)])  3.15 us
    ppermute x1, waiting for transfers between devices, swapped_sum(): lax.ppermute(value, axis, [(i, i ^ step) for i in range(size)])  3.05 us
    ppermute x1, starting transfers between devices, body(): other = lax.ppermute(sums, 'rep', [(i, i ^ 1) for i in range(rep_count)])  2.42 us
    reshape x1, other arithmetic, body(): exchange = (sums[:held] + other[:held]).reshape(own_count, box_edge, plane)  1.58 us
  transfers between devices with their start and end apart: 9, of which 6 were waited for; matrix products, arithmetic and copies ran while one was open for 4% of the time, Pallas kernels for 0%

profile of v4, /device:TPU:0, one launch (start us, length us, event | category | flops | bytes accessed | tf_op | source)
XLA Modules:
  0.0 39.2 jit_solution(8842132090664066040)
XLA Ops:
  0.6 1.5 %collective-permute-start = (bf16[1,32,1024]{2,1,0:T(8,128)(2,1)}, bf16[1,32,1024]{2,1,0:T(8,128)(2,1)S(1)}, u32[]{:S(2)}, u32[]{:S(2)}) collective-permute-start(bf16[1,32,1024]{2,1,0:T(8,128)(2,1)} %refs_2_.1), channel_id=1, source_target_pairs={{0,0},{1,2},{2,1},{3,3},{4,4},{5,6},{6,5},{7,7},{8,8},{9,10},{10,9... | collective-permute-start | bytes 196616 | tf_op jit(solution)/shard_map/ppermute | solution.py:53
  2.1 3.1 %collective-permute-start.1 = (bf16[1,32,1024]{2,1,0:T(8,128)(2,1)}, bf16[1,32,1024]{2,1,0:T(8,128)(2,1)S(1)}, u32[]{:S(2)}, u32[]{:S(2)}) collective-permute-start(bf16[1,32,1024]{2,1,0:T(8,128)(2,1)} %refs_2_.1), channel_id=1, source_target_pairs={{0,4},{1,6},{2,5},{3,7},{4,8},{5,10},{6,9},{7,11},{8,12},{9,14},{1... | collective-permute-start | bytes 196616 | tf_op jit(solution)/shard_map/ppermute | solution.py:53
  5.2 2.6 %collective-permute-start.2 = (bf16[1,32,1024]{2,1,0:T(8,128)(2,1)}, bf16[1,32,1024]{2,1,0:T(8,128)(2,1)S(1)}, u32[]{:S(2)}, u32[]{:S(2)}) collective-permute-start(bf16[1,32,1024]{2,1,0:T(8,128)(2,1)} %refs_2_.1), channel_id=1, source_target_pairs={{0,8},{1,10},{2,9},{3,11},{4,12},{5,14},{6,13},{7,15},{8,0},{9,2},... | collective-permute-start | bytes 196616 | tf_op jit(solution)/shard_map/ppermute | solution.py:53
  7.8 1.3 %collective-permute-start.3 = (bf16[1,32,1024]{2,1,0:T(8,128)(2,1)}, bf16[1,32,1024]{2,1,0:T(8,128)(2,1)S(1)}, u32[]{:S(2)}, u32[]{:S(2)}) collective-permute-start(bf16[1,32,1024]{2,1,0:T(8,128)(2,1)} %refs_2_.1), channel_id=1, source_target_pairs={{0,12},{1,14},{2,13},{3,15},{4,0},{5,2},{6,1},{7,3},{8,4},{9,6},{1... | collective-permute-start | bytes 196616 | tf_op jit(solution)/shard_map/ppermute | solution.py:53
  9.1 0.0 collective-permute-done.refs_6_
  9.1 0.0 copy-start
  9.1 0.5 %collective-permute-done.1.refs_7_ = bf16[1,32,1024]{2,1,0:T(8,128)(2,1)S(1)} collective-permute-done((bf16[1,32,1024]{2,1,0:T(8,128)(2,1)}, bf16[1,32,1024]{2,1,0:T(8,128)(2,1)S(1)}, u32[]{:S(2)}, u32[]{:S(2)}) %collective-permute-start.1) | collective-permute-done | bytes 65568 | tf_op jit(solution)/shard_map/ppermute | solution.py:53
  9.7 0.0 copy-start.1
  9.7 2.5 %collective-permute-done.2.refs_8_ = bf16[1,32,1024]{2,1,0:T(8,128)(2,1)S(1)} collective-permute-done((bf16[1,32,1024]{2,1,0:T(8,128)(2,1)}, bf16[1,32,1024]{2,1,0:T(8,128)(2,1)S(1)}, u32[]{:S(2)}, u32[]{:S(2)}) %collective-permute-start.2) | collective-permute-done | bytes 65568 | tf_op jit(solution)/shard_map/ppermute | solution.py:53
  12.2 0.0 copy-start.2
  12.2 0.7 %collective-permute-done.3.refs_9_ = bf16[1,32,1024]{2,1,0:T(8,128)(2,1)S(1)} collective-permute-done((bf16[1,32,1024]{2,1,0:T(8,128)(2,1)}, bf16[1,32,1024]{2,1,0:T(8,128)(2,1)S(1)}, u32[]{:S(2)}, u32[]{:S(2)}) %collective-permute-start.3) | collective-permute-done | bytes 65568 | tf_op jit(solution)/shard_map/ppermute | solution.py:53
  12.8 0.0 copy-start.3
  12.9 0.0 copy-done
  12.9 0.0 copy-done.1
  12.9 0.0 copy-done.2
  12.9 0.6 %copy-done.3 = bf16[1,32,1024]{2,1,0:T(8,128)(2,1)} copy-done((bf16[1,32,1024]{2,1,0:T(8,128)(2,1)}, bf16[1,32,1024]{2,1,0:T(8,128)(2,1)S(1)}, u32[]{:S(2)}) %copy-start.3) | copy-done | bytes 65560
  13.5 6.3 %pairs.1 = f32[40,1024]{1,0:T(8,128)} custom-call(s32[1,24]{1,0:T(1,128)} %refs_0_.1, s32[3,8]{1,0:T(4,128)} %bitcast.4, bf16[1,32,1024]{2,1,0:T(8,128)(2,1)} %refs_2_.1, f32[32,1024]{1,0:T(8,128)} %refs_3_.1, bf16[2,3,256,512]{3,2,1,0:T(8,128)(2,1)} %constant.8.clone.refs_4_, bf16[2,2,256,256]{3,2,1,0:T(8,128)(2,1)} %constant.9.clone.refs_5_, ...), custom_call_target="tpu_custom_call" | custom-call | tf_op jit(solution)/shard_map/pairs/pallas_call | solution.py:278
  19.8 2.4 %collective-permute-start.4 = (f32[40,1024]{1,0:T(8,128)}, f32[40,1024]{1,0:T(8,128)S(1)}, u32[]{:S(2)}, u32[]{:S(2)}) collective-permute-start(f32[40,1024]{1,0:T(8,128)} %pairs.1), channel_id=1, source_target_pairs={{0,1},{1,0},{2,3},{3,2},{4,5},{5,4},{6,7},{7,6},{8,9},{9,8},{10,11... | collective-permute-start | bytes 491528 | tf_op jit(solution)/shard_map/ppermute | solution.py:298
  22.2 1.2 %collective-permute-done.4 = f32[40,1024]{1,0:T(8,128)S(1)} collective-permute-done((f32[40,1024]{1,0:T(8,128)}, f32[40,1024]{1,0:T(8,128)S(1)}, u32[]{:S(2)}, u32[]{:S(2)}) %collective-permute-start.4) | collective-permute-done | bytes 163872 | tf_op jit(solution)/shard_map/ppermute | solution.py:298
  23.5 0.7 %slice_add_fusion.1 = f32[8,128]{1,0:T(8,128)S(1)} fusion(f32[40,1024]{1,0:T(8,128)S(1)} %collective-permute-done.4, f32[40,1024]{1,0:T(8,128)} %pairs.1), kind=kLoop, calls=%fused_computation.2 | loop fusion | flops 1024 | bytes 12288 | tf_op jit(solution)/shard_map/add | solution.py:299
  24.2 0.6 %collective-permute-start.5 = (f32[8,128]{1,0:T(8,128)S(1)}, f32[8,128]{1,0:T(8,128)S(1)}, u32[]{:S(2)}, u32[]{:S(2)}) collective-permute-start(f32[8,128]{1,0:T(8,128)S(1)} %slice_add_fusion.1), channel_id=1, source_target_pairs={{0,2},{2,0},{1,3},{3,1},{4,6},{6,4},{5,7},{7,5},{8,10},{10,8},{9,1... | collective-permute-start | bytes 12296 | tf_op jit(solution)/shard_map/ppermute | solution.py:37
  24.7 3.1 %collective-permute-done.5 = f32[8,128]{1,0:T(8,128)S(1)} collective-permute-done((f32[8,128]{1,0:T(8,128)S(1)}, f32[8,128]{1,0:T(8,128)S(1)}, u32[]{:S(2)}, u32[]{:S(2)}) %collective-permute-start.5) | collective-permute-done | bytes 4128 | tf_op jit(solution)/shard_map/ppermute | solution.py:37
  27.8 0.2 collective-permute-start.6
  28.0 3.5 %collective-permute-start.7 = (f32[8,128]{1,0:T(8,128)S(1)}, f32[8,128]{1,0:T(8,128)S(1)}, u32[]{:S(2)}, u32[]{:S(2)}) collective-permute-start(f32[8,128]{1,0:T(8,128)S(1)} %add.20), channel_id=1, source_target_pairs={{0,8},{4,12},{8,0},{12,4},{1,9},{5,13},{9,1},{13,5},{2,10},{6,14},... | collective-permute-start | bytes 12296 | tf_op jit(solution)/shard_map/ppermute | solution.py:31
  31.5 0.7 %collective-permute-start.8 = (f32[8,128]{1,0:T(8,128)S(1)}, f32[8,128]{1,0:T(8,128)S(1)}, u32[]{:S(2)}, u32[]{:S(2)}) collective-permute-start(f32[8,128]{1,0:T(8,128)S(1)} %add.20), channel_id=1, source_target_pairs={{0,12},{4,8},{8,4},{12,0},{1,13},{5,9},{9,5},{13,1},{2,14},{6,10},... | collective-permute-start | bytes 12296 | tf_op jit(solution)/shard_map/ppermute | solution.py:31
  32.2 1.6 %fusion = f32[1,32,1024]{2,1,0:T(8,128)} fusion(f32[40,1024]{1,0:T(8,128)S(1)} %collective-permute-done.4, f32[40,1024]{1,0:T(8,128)} %pairs.1), kind=kLoop, calls=%fused_computation.1 | loop fusion | flops 32768 | bytes 393216 | tf_op jit(solution)/shard_map/reshape | solution.py:300
  33.7 0.0 collective-permute-done.6
  33.7 0.0 collective-permute-done.7
  33.7 3.1 %collective-permute-done.8 = f32[8,128]{1,0:T(8,128)S(1)} collective-permute-done((f32[8,128]{1,0:T(8,128)S(1)}, f32[8,128]{1,0:T(8,128)S(1)}, u32[]{:S(2)}, u32[]{:S(2)}) %collective-permute-start.8) | collective-permute-done | bytes 4128 | tf_op jit(solution)/shard_map/ppermute | solution.py:31
  36.9 0.5 %slice.19 = f32[1,1]{1,0:T(1,128)} slice(f32[8,128]{1,0:T(8,128)S(1)} %add_add_fusion), slice={[0:1], [0:1]} | slice | bytes 8 | tf_op jit(solution)/shard_map/slice | solution.py:301
  (2 shorter events, 0.0 us)
Async XLA Ops:
  0.6 8.5 %collective-permute-start = (bf16[1,32,1024]{2,1,0:T(8,128)(2,1)}, bf16[1,32,1024]{2,1,0:T(8,128)(2,1)S(1)}, u32[]{:S(2)}, u32[]{:S(2)}) collective-permute-start(bf16[1,32,1024]{2,1,0:T(8,128)(2,1)} %refs_2_.1), channel_id=1, source_target_pairs={{0,0},{1,2},{2,1},{3,3},{4,4},{5,6},{6,5},{7,7},{8,8},{9,10},{10,9... | collective-permute-start | bytes 196616 | tf_op jit(solution)/shard_map/ppermute | solution.py:53
  2.1 7.5 %collective-permute-start.1 = (bf16[1,32,1024]{2,1,0:T(8,128)(2,1)}, bf16[1,32,1024]{2,1,0:T(8,128)(2,1)S(1)}, u32[]{:S(2)}, u32[]{:S(2)}) collective-permute-start(bf16[1,32,1024]{2,1,0:T(8,128)(2,1)} %refs_2_.1), channel_id=1, source_target_pairs={{0,4},{1,6},{2,5},{3,7},{4,8},{5,10},{6,9},{7,11},{8,12},{9,14},{1... | collective-permute-start | bytes 196616 | tf_op jit(solution)/shard_map/ppermute | solution.py:53
  5.2 7.0 %collective-permute-start.2 = (bf16[1,32,1024]{2,1,0:T(8,128)(2,1)}, bf16[1,32,1024]{2,1,0:T(8,128)(2,1)S(1)}, u32[]{:S(2)}, u32[]{:S(2)}) collective-permute-start(bf16[1,32,1024]{2,1,0:T(8,128)(2,1)} %refs_2_.1), channel_id=1, source_target_pairs={{0,8},{1,10},{2,9},{3,11},{4,12},{5,14},{6,13},{7,15},{8,0},{9,2},... | collective-permute-start | bytes 196616 | tf_op jit(solution)/shard_map/ppermute | solution.py:53
  7.8 5.1 %collective-permute-start.3 = (bf16[1,32,1024]{2,1,0:T(8,128)(2,1)}, bf16[1,32,1024]{2,1,0:T(8,128)(2,1)S(1)}, u32[]{:S(2)}, u32[]{:S(2)}) collective-permute-start(bf16[1,32,1024]{2,1,0:T(8,128)(2,1)} %refs_2_.1), channel_id=1, source_target_pairs={{0,12},{1,14},{2,13},{3,15},{4,0},{5,2},{6,1},{7,3},{8,4},{9,6},{1... | collective-permute-start | bytes 196616 | tf_op jit(solution)/shard_map/ppermute | solution.py:53
  9.1 3.7 %copy-start = (bf16[1,32,1024]{2,1,0:T(8,128)(2,1)}, bf16[1,32,1024]{2,1,0:T(8,128)(2,1)S(1)}, u32[]{:S(2)}) copy-start(bf16[1,32,1024]{2,1,0:T(8,128)(2,1)S(1)} %collective-permute-done.refs_6_) | copy-start | bytes 196612
  9.7 3.2 %copy-start.1 = (bf16[1,32,1024]{2,1,0:T(8,128)(2,1)}, bf16[1,32,1024]{2,1,0:T(8,128)(2,1)S(1)}, u32[]{:S(2)}) copy-start(bf16[1,32,1024]{2,1,0:T(8,128)(2,1)S(1)} %collective-permute-done.1.refs_7_) | copy-start | bytes 196612
  12.2 0.7 %copy-start.2 = (bf16[1,32,1024]{2,1,0:T(8,128)(2,1)}, bf16[1,32,1024]{2,1,0:T(8,128)(2,1)S(1)}, u32[]{:S(2)}) copy-start(bf16[1,32,1024]{2,1,0:T(8,128)(2,1)S(1)} %collective-permute-done.2.refs_8_) | copy-start | bytes 196612
  12.8 0.6 %copy-start.3 = (bf16[1,32,1024]{2,1,0:T(8,128)(2,1)}, bf16[1,32,1024]{2,1,0:T(8,128)(2,1)S(1)}, u32[]{:S(2)}) copy-start(bf16[1,32,1024]{2,1,0:T(8,128)(2,1)S(1)} %collective-permute-done.3.refs_9_) | copy-start | bytes 196612
  19.8 3.7 %collective-permute-start.4 = (f32[40,1024]{1,0:T(8,128)}, f32[40,1024]{1,0:T(8,128)S(1)}, u32[]{:S(2)}, u32[]{:S(2)}) collective-permute-start(f32[40,1024]{1,0:T(8,128)} %pairs.1), channel_id=1, source_target_pairs={{0,1},{1,0},{2,3},{3,2},{4,5},{5,4},{6,7},{7,6},{8,9},{9,8},{10,11... | collective-permute-start | bytes 491528 | tf_op jit(solution)/shard_map/ppermute | solution.py:298
  24.2 3.6 %collective-permute-start.5 = (f32[8,128]{1,0:T(8,128)S(1)}, f32[8,128]{1,0:T(8,128)S(1)}, u32[]{:S(2)}, u32[]{:S(2)}) collective-permute-start(f32[8,128]{1,0:T(8,128)S(1)} %slice_add_fusion.1), channel_id=1, source_target_pairs={{0,2},{2,0},{1,3},{3,1},{4,6},{6,4},{5,7},{7,5},{8,10},{10,8},{9,1... | collective-permute-start | bytes 12296 | tf_op jit(solution)/shard_map/ppermute | solution.py:37
  27.8 6.0 %collective-permute-start.6 = (f32[8,128]{1,0:T(8,128)S(1)}, f32[8,128]{1,0:T(8,128)S(1)}, u32[]{:S(2)}, u32[]{:S(2)}) collective-permute-start(f32[8,128]{1,0:T(8,128)S(1)} %add.20), channel_id=1, source_target_pairs={{0,4},{4,0},{8,12},{12,8},{1,5},{5,1},{9,13},{13,9},{2,6},{6,2},{1... | collective-permute-start | bytes 12296 | tf_op jit(solution)/shard_map/ppermute | solution.py:31
  28.0 5.8 %collective-permute-start.7 = (f32[8,128]{1,0:T(8,128)S(1)}, f32[8,128]{1,0:T(8,128)S(1)}, u32[]{:S(2)}, u32[]{:S(2)}) collective-permute-start(f32[8,128]{1,0:T(8,128)S(1)} %add.20), channel_id=1, source_target_pairs={{0,8},{4,12},{8,0},{12,4},{1,9},{5,13},{9,1},{13,5},{2,10},{6,14},... | collective-permute-start | bytes 12296 | tf_op jit(solution)/shard_map/ppermute | solution.py:31
  31.5 5.4 %collective-permute-start.8 = (f32[8,128]{1,0:T(8,128)S(1)}, f32[8,128]{1,0:T(8,128)S(1)}, u32[]{:S(2)}, u32[]{:S(2)}) collective-permute-start(f32[8,128]{1,0:T(8,128)S(1)} %add.20), channel_id=1, source_target_pairs={{0,12},{4,8},{8,4},{12,0},{1,13},{5,9},{9,5},{13,1},{2,14},{6,10},... | collective-permute-start | bytes 12296 | tf_op jit(solution)/shard_map/ppermute | solution.py:31
